TPU v7x, 32 devices: a whole 2x2x4 slice. The times are simulated.
32 devices in a mesh: member: 2 (over x), wave: 16 (over z, y, core).
Axes of the slice: x: 2, y: 2, z: 4, core: 2. Of those that a mesh axis runs over, the one named last changes fastest.
Arguments:
- spectral: bfloat16 [1024, 2, 256, 192], P(('member', 'wave')), parts along dimension 0, may hold values from -6 to 6
- basis: bfloat16 [512, 2, 256, 256], P('wave'), may hold values from -0.25 to 0.25
- quad_weights: float32 [256], replicated, may hold values from 0.5 to 2
- column: float32 [96, 96], replicated, may hold values from -0.625 to 0.625
- square_coef: float32 [96], replicated, may hold values from -0.3 to 0.3
- cube_coef: float32 [96], replicated, may hold values from 0.05 to 0.2
- trunc: int32 [256], replicated, may hold values from 16 to 512, as said below
Outputs:
- new_spectral: bfloat16 [1024, 2, 256, 192], P(('member', 'wave')), parts along dimension 0
There are 2 independent parts, one for each index of `member`. A program takes and returns all parts, laid end to end along the dimension named above; an argument that names none is the same for every part. Nothing has to cross between parts.
Inputs may be any that keep to these rules, and one draw needn't show every extreme that they name: `trunc`: rows nearer the equator never keep fewer wavenumbers than rows nearer the pole.
All inputs are finite; a program needn't handle non-finite values.
Results may differ from a plain program's by a relative error of at most 0.0057.
Values may be sent and summed in bfloat16 or wider, within the bound.
No kernel may reach another device: no remote copies, remote signals or barrier semaphores. Data moves between devices by JAX's collectives and lax.ppermute only.
A program may use at most 128 MiB of HBM per device.

v0:
```python
import functools
import math

import jax
import jax.numpy as jnp
from jax import lax
from jax.experimental import pallas as pl
from jax.experimental.pallas import tpu as pltpu
from jax.sharding import PartitionSpec as P


NLON = 1024
LANES = 128
F32 = jnp.float32
BF16 = jnp.bfloat16
STEPS = 2
VMEM_LIMIT = 56 * 1024 * 1024


def params():
    return pltpu.CompilerParams(
        dimension_semantics=("arbitrary",), vmem_limit_bytes=VMEM_LIMIT
    )


def owned_groups(devices):
    turn = (0, 3, 1, 2) if devices % 4 == 0 else tuple(range(devices))
    size = len(turn)
    return [devices - 1 - (e // size * size + turn[e % size]) for e in range(devices)]


def latitude_order(half_lats, devices):
    rows = half_lats // devices
    pairs = rows // 2
    lane = jnp.arange(half_lats, dtype=jnp.int32)
    half = lane // (half_lats // 2)
    owner = lane % (half_lats // 2) // pairs
    pair = lane % pairs
    groups = jnp.array(owned_groups(devices), dtype=jnp.int32)
    group = jnp.sum(jnp.where(owner[:, None] == jnp.arange(devices), groups[None, :], 0), axis=1)
    return group * rows + half * pairs + pair


def exchange_order(devices):
    quarter = max(1, devices // 4)
    order = [0]
    for t in range(quarter):
        order += [2 * quarter + t, quarter + t, 3 * quarter + t]
    return order + list(range(quarter - 1, 0, -1))


def forward_kernel(devices, group, waves, pos_ref, spec_ref, basis_ref, trunc_ref, perm_ref, *rest):
    outs, fold = rest[:devices], rest[devices:]
    pos = pos_ref[0]
    levels = outs[0].shape[3] // 4
    half_slots = spec_ref.shape[3]
    tiles = 4 * levels // LANES
    jj = perm_ref.shape[1] // 2
    pairs = jj // devices
    first = pos * waves + pl.program_id(0) * group
    slot = 2 * lax.broadcasted_iota(jnp.int32, (1, half_slots), 1)
    trunc = trunc_ref[...]

    def one(m, carry):
        wave = first + m
        parity = []
        for p in range(2):
            spec = spec_ref[m, p]
            spec = jnp.where(slot + (wave + p) < 2 * half_slots, spec, jnp.zeros_like(spec))
            parity.append(jnp.dot(spec, basis_ref[m, p], preferred_element_type=F32))
        both = jnp.concatenate([parity[0] + parity[1], parity[0] - parity[1]], axis=0)
        both = jnp.where(trunc > wave, both, 0.0).astype(BF16)
        both = jnp.dot(both, perm_ref[...], preferred_element_type=F32)
        for r in range(2):
            rows = []
            for half in range(2):
                for hemi in range(2):
                    at = (2 * hemi + r) * levels
                    rows.append(both[at : at + levels, half * jj : (half + 1) * jj])
            turned = jnp.concatenate(rows, axis=0).T
            for t in range(tiles):
                at = pl.ds(m, jj, stride=group)
                fold[r * tiles + t][at, :] = turned[:, t * LANES : (t + 1) * LANES]
        return carry

    lax.fori_loop(0, group, one, 0, unroll=group)
    size = pairs * group
    for i, s in enumerate(exchange_order(devices)):
        at = pl.multiple_of((pos ^ s) * size, 8)
        for r in range(2):
            for t in range(tiles):
                block = fold[r * tiles + t][pl.ds(at, size), :].reshape(pairs, group, LANES)
                outs[i][:, r, :, t * LANES : (t + 1) * LANES] = block.astype(BF16)


def forward(pos, spec, basis, trunc, perm, devices):
    waves, _, channels, half_slots = spec.shape
    half_lats = basis.shape[3]
    group = min(8, waves)
    pairs = half_lats // (2 * devices)
    lanes = 2 * channels
    return pl.pallas_call(
        functools.partial(forward_kernel, devices, group, waves),
        grid_spec=pltpu.PrefetchScalarGridSpec(
            num_scalar_prefetch=1,
            grid=(waves // group,),
            in_specs=[
                pl.BlockSpec((group, 2, channels, half_slots), lambda i, s: (i, 0, 0, 0)),
                pl.BlockSpec((group, 2, half_slots, half_lats), lambda i, s: (i, 0, 0, 0)),
                pl.BlockSpec((1, half_lats), lambda i, s: (0, 0)),
                pl.BlockSpec((half_lats, half_lats), lambda i, s: (0, 0)),
            ],
            out_specs=[pl.BlockSpec((pairs, 2, group, lanes), lambda i, s: (0, 0, i, 0))] * devices,
            scratch_shapes=[pltpu.VMEM((half_lats // 2 * group, LANES), F32)] * (2 * lanes // LANES),
        ),
        out_shape=[jax.ShapeDtypeStruct((pairs, 2, waves, lanes), BF16)] * devices,
        compiler_params=params(),
        name="forward",
    )(pos, spec, basis, trunc, perm)


def grid_kernel(devices, waves, unroll, pos_ref, cos_ref, sin_ref, mid_ref, mix_ref, coef_ref, *rest):
    blocks, outs = rest[:devices], rest[devices : 2 * devices]
    mean_ref, coeffs, plus, minus, even, odd = rest[2 * devices :]
    pos = pos_ref[0]
    total = devices * waves
    count, lanes = blocks[0].shape[0], blocks[0].shape[3]
    width = count * lanes
    order = exchange_order(devices)
    for i, s in enumerate(order):
        at = pl.multiple_of((pos ^ s) * waves, 8)
        for r in range(2):
            for c in range(count):
                part = blocks[i][c, r]
                coeffs[pl.ds(r * total + at, waves), c * lanes : (c + 1) * lanes] = part
    half = cos_ref.shape[0]
    step = half // STEPS
    scale = 1.0 / math.sqrt(total)
    middle = jnp.dot(mid_ref[...], coeffs[:total, :], preferred_element_type=F32)[0:1]
    row = lax.broadcasted_iota(jnp.int32, (step, 1), 0)

    def tendency(temp):
        values = []
        for c in range(count):
            mine = temp[:, c * lanes : (c + 1) * lanes]
            mixed = jnp.dot(mine.astype(BF16), mix_ref[...], preferred_element_type=F32)
            values.append(mixed + mine * mine * (coef_ref[0:1, :] - coef_ref[1:2, :] * mine))
        return jnp.concatenate(values, axis=1)

    def one(t, total_sum):
        at = pl.multiple_of(t * step, step)
        cosine = jnp.dot(
            cos_ref[pl.ds(at, step), :], coeffs[:total, :], preferred_element_type=F32
        )
        sine = jnp.dot(
            sin_ref[pl.ds(at, step), :], coeffs[total:, :], preferred_element_type=F32
        )
        first = tendency(scale * (cosine + sine))
        last = tendency(scale * jnp.where(row + at == 0, middle, cosine - sine))
        plus[pl.ds(at, step), :] = first
        minus[pl.ds(at, step), :] = last
        return total_sum + jnp.sum(first + last, axis=0, keepdims=True)

    mean = lax.fori_loop(0, STEPS, one, jnp.zeros((1, width), F32), unroll=unroll)
    mean = mean * (0.5 / half)
    mean_ref[0] = jnp.broadcast_to(mean, mean_ref.shape[1:])
    centre = minus[0:1, :] - mean

    def two(t, carry):
        at = pl.multiple_of(t * step, step)
        first = plus[pl.ds(at, step), :] - mean
        last = jnp.where(row + at == 0, 0.0, minus[pl.ds(at, step), :] - mean)
        even[pl.ds(at, step), :] = (first + last).astype(BF16)
        odd[pl.ds(at, step), :] = (first - last).astype(BF16)
        return carry

    lax.fori_loop(0, STEPS, two, 0, unroll=unroll)
    sign = (1 - 2 * (row % 2)).astype(F32)
    gain = math.sqrt(1.0 / half)

    def three(t, carry):
        at = pl.multiple_of(t * step, step)
        cosine = jnp.dot(cos_ref[pl.ds(at, step), :], even[...], preferred_element_type=F32)
        coeffs[pl.ds(at, step), :] = (gain * (cosine + sign * centre)).astype(BF16)
        sine = jnp.dot(sin_ref[pl.ds(at, step), :], odd[...], preferred_element_type=F32)
        coeffs[pl.ds(total + at, step), :] = (gain * sine).astype(BF16)
        return carry

    lax.fori_loop(0, STEPS, three, 0, unroll=unroll)
    for i, s in enumerate(order):
        at = pl.multiple_of((pos ^ s) * waves, 8)
        for r in range(2):
            for c in range(count):
                part = coeffs[pl.ds(r * total + at, waves), c * lanes : (c + 1) * lanes]
                outs[i][c, r] = part


def on_grid(pos, cosine, sine, middle, mix, coef, blocks, unroll):
    devices = len(blocks)
    pairs, _, waves, lanes = blocks[0].shape
    half, total = cosine.shape
    assert half == total == devices * waves
    count = 2 if pairs % 2 == 0 else 1
    width = count * lanes
    block = pl.BlockSpec((count, 2, waves, lanes), lambda q, s: (q, 0, 0, 0))
    whole = lambda q, s: (0, 0)
    return pl.pallas_call(
        functools.partial(grid_kernel, devices, waves, unroll),
        grid_spec=pltpu.PrefetchScalarGridSpec(
            num_scalar_prefetch=1,
            grid=(pairs // count,),
            in_specs=[
                pl.BlockSpec((half, total), whole),
                pl.BlockSpec((half, total), whole),
                pl.BlockSpec((8, total), whole),
                pl.BlockSpec((lanes, lanes), whole),
                pl.BlockSpec((2, lanes), whole),
            ]
            + [block] * devices,
            out_specs=[block] * devices + [pl.BlockSpec((1, 8, width), lambda q, s: (q, 0, 0))],
            scratch_shapes=[
                pltpu.VMEM((2 * total, width), BF16),
                pltpu.VMEM((half, width), F32),
                pltpu.VMEM((half, width), F32),
                pltpu.VMEM((half, width), BF16),
                pltpu.VMEM((half, width), BF16),
            ],
        ),
        out_shape=[jax.ShapeDtypeStruct(blocks[0].shape, BF16)] * devices
        + [jax.ShapeDtypeStruct((pairs // count, 8, width), F32)],
        compiler_params=params(),
        name="grid",
    )(pos, cosine, sine, middle, mix, coef, *blocks)


def inverse_kernel(
    devices, group, waves, unroll, pos_ref, sums_ref, spec_ref, basis_ref, trunc_ref, weight_ref, perm_ref,
    share_ref, *rest
):
    blocks = rest[:devices]
    out_ref, fold = rest[devices], rest[devices + 1 :]
    pos = pos_ref[0]
    levels = blocks[0].shape[3] // 4
    half_slots = spec_ref.shape[3]
    jj = perm_ref.shape[0] // 2
    pairs = jj // devices
    tiles = 4 * levels // LANES
    size = pairs * group
    for i, s in enumerate(exchange_order(devices)):
        at = pl.multiple_of((pos ^ s) * size, 8)
        for r in range(2):
            for t in range(tiles):
                block = blocks[i][:, r, :, t * LANES : (t + 1) * LANES].astype(F32)
                fold[r * tiles + t][pl.ds(at, size), :] = block.reshape(size, LANES)
    first = pos * waves + pl.program_id(0) * group
    slot = 2 * lax.broadcasted_iota(jnp.int32, (1, half_slots), 1)
    trunc = trunc_ref[...]
    weight = weight_ref[...]

    def one(m, carry):
        wave = first + m
        turned = []
        for r in range(2):
            at = pl.ds(m, jj, stride=group)
            total = sums_ref[r * waves + pl.program_id(0) * group + m]
            columns = []
            for t in range(tiles):
                share = total * share_ref[:, t * LANES : (t + 1) * LANES]
                columns.append((fold[r * tiles + t][at, :] + share).T)
            turned.append(jnp.concatenate(columns, axis=0))
        rows = []
        for hemi in range(2):
            for r in range(2):
                pieces = []
                for half in range(2):
                    at = (2 * half + hemi) * levels
                    pieces.append(turned[r][at : at + levels])
                rows.append(jnp.concatenate(pieces, axis=1))
        both = jnp.concatenate(rows, axis=0).astype(BF16)
        both = jnp.dot(both, perm_ref[...], preferred_element_type=F32)
        both = jnp.where(trunc > wave, both, 0.0)
        channels = 2 * levels
        north, south = both[:channels], both[channels:]
        for p in range(2):
            folded = (weight * (north + south if p == 0 else north - south)).astype(BF16)
            direct = lax.dot_general(
                folded, basis_ref[m, p], (((1,), (1,)), ((), ())), preferred_element_type=F32
            )
            value = spec_ref[m, p].astype(F32) + direct
            out_ref[m, p] = jnp.where(slot + (wave + p) < 2 * half_slots, value, 0.0).astype(BF16)
        return carry

    lax.fori_loop(0, group, one, 0, unroll=min(group, unroll))


def inverse(pos, sums, spec, basis, trunc, weight, perm, share, blocks, unroll):
    devices = len(blocks)
    waves, _, channels, half_slots = spec.shape
    half_lats = basis.shape[3]
    group = min(8, waves)
    pairs = half_lats // (2 * devices)
    lanes = 2 * channels
    return pl.pallas_call(
        functools.partial(inverse_kernel, devices, group, waves, unroll),
        grid_spec=pltpu.PrefetchScalarGridSpec(
            num_scalar_prefetch=1,
            grid=(waves // group,),
            in_specs=[
                pl.BlockSpec(memory_space=pltpu.SMEM),
                pl.BlockSpec((group, 2, channels, half_slots), lambda i, s: (i, 0, 0, 0)),
                pl.BlockSpec((group, 2, half_slots, half_lats), lambda i, s: (i, 0, 0, 0)),
                pl.BlockSpec((1, half_lats), lambda i, s: (0, 0)),
                pl.BlockSpec((1, half_lats), lambda i, s: (0, 0)),
                pl.BlockSpec((half_lats, half_lats), lambda i, s: (0, 0)),
                pl.BlockSpec((half_lats // 2, lanes), lambda i, s: (0, 0)),
            ]
            + [pl.BlockSpec((pairs, 2, group, lanes), lambda i, s: (0, 0, i, 0))] * devices,
            out_specs=pl.BlockSpec((group, 2, channels, half_slots), lambda i, s: (i, 0, 0, 0)),
            scratch_shapes=[pltpu.VMEM((half_lats // 2 * group, LANES), F32)] * (2 * lanes // LANES),
        ),
        out_shape=jax.ShapeDtypeStruct(spec.shape, BF16),
        compiler_params=params(),
        name="inverse",
    )(pos, sums, spec, basis, trunc, weight, perm, share, *blocks)


def cos_sin(rows, columns):
    phases = rows[:, None] * columns[None, :] % NLON
    angles = phases.astype(F32) * (2.0 * math.pi / NLON)
    return jnp.cos(angles), jnp.sin(angles)


def fourier_tables(size):
    low = 32
    col = jnp.arange(size, dtype=jnp.int32)
    c0, s0, c1, s1 = lax.optimization_barrier(
        cos_sin(jnp.arange(low, dtype=jnp.int32), col)
        + cos_sin(low * jnp.arange(size // low, dtype=jnp.int32), col)
    )
    cos = c1[:, None] * c0[None] - s1[:, None] * s0[None]
    sin = s1[:, None] * c0[None] + c1[:, None] * s0[None]
    return cos.reshape(size, size).astype(BF16), (-sin).reshape(size, size).astype(BF16)


def exchange(arrays, devices, needed):
    got = [arrays[0]]
    for array, s in list(zip(arrays, exchange_order(devices)))[1:]:
        pairs = [(i, i ^ s) for i in range(devices) if needed(i, i ^ s)]
        got.append(lax.ppermute(array, "wave", pairs))
    return got


def per_device(spectral, basis, quad_weights, column, square_coef, cube_coef, trunc):
    devices = lax.axis_size("wave")
    position = lax.axis_index("wave").astype(jnp.int32)
    waves, _, _, channels = spectral.shape
    half_lats = basis.shape[3]
    levels = channels // 2
    rows = half_lats // devices
    pairs = rows // 2
    pos = position.reshape(1)
    spec = jnp.swapaxes(spectral, 2, 3)
    order = latitude_order(half_lats, devices)
    lats = jnp.arange(half_lats, dtype=jnp.int32)
    perm = (lats[:, None] == order[None, :]).astype(BF16)
    back = (order[:, None] == lats[None, :]).astype(BF16)
    trunc_row = trunc.reshape(1, half_lats)
    weight_row = quad_weights.reshape(1, half_lats)
    blocks = forward(pos, spec, basis, trunc_row, perm, devices)

    groups = owned_groups(devices)
    reach = [min(devices, g + 1 + max(1, devices // 16)) for g in range(devices)]
    top = jnp.max(trunc.reshape(devices, rows), axis=1)
    fits = jnp.all(top <= waves * jnp.array(reach, dtype=jnp.int32))

    def finish(sparse, blocks):
        def there(source, owner):
            return not sparse or source < reach[groups[owner]]

        def home(owner, source):
            return there(source, owner)

        total = devices * waves
        cosine, sine = fourier_tables(total)
        sign = 1 - 2 * (jnp.arange(total, dtype=jnp.int32) % 2)
        middle = jnp.broadcast_to(sign.astype(BF16), (8, total))
        mix = jnp.kron(jnp.eye(4, dtype=F32), column.T).astype(BF16)
        coef = jnp.stack([jnp.tile(square_coef, 4), jnp.tile(cube_coef, 4)])
        sums = 2.0 * jnp.sum(cosine.astype(F32), axis=1) - cosine[:, 0].astype(F32)
        sums = jnp.stack([sums + sign.astype(F32), jnp.zeros((total,), F32)])
        kept = lax.dynamic_slice(sums, (0, position * waves), (2, waves)).reshape(-1)
        held = quad_weights.reshape(devices, 2, pairs)
        held = jnp.swapaxes(jnp.stack([held[g] for g in groups]), 1, 2)
        held = held.reshape(devices * pairs, 2, 1, 1) / (2.0 * jnp.sum(quad_weights))

        got = exchange(blocks, devices, there)
        *parts, means = on_grid(
            pos, cosine, sine, middle, mix, coef, got, STEPS if sparse else 1
        )
        parts = exchange(parts, devices, home)

        sent = means[:, 0].reshape(1, -1, LANES)
        sent = jnp.broadcast_to(sent, (devices,) + sent.shape[1:])
        every = lax.all_to_all(sent, "wave", split_axis=0, concat_axis=0, tiled=True)
        every = every.reshape(devices * pairs, 4 * levels)
        level_mean = jnp.sum(held * every.reshape(-1, 2, 2, levels), axis=(0, 1, 2))
        share = math.sqrt(2.0 / NLON) * (every - jnp.tile(level_mean, 4))
        return inverse(
            pos, kept, spec, basis, trunc_row, weight_row, back, share, parts,
            8 if sparse else 1,
        )

    def sparse(blocks):
        return finish(True, blocks)

    def dense(blocks):
        return finish(False, blocks)

    out = lax.cond(fits, sparse, dense, blocks)
    return jnp.swapaxes(out, 2, 3)


def solution(mesh):
    return jax.shard_map(
        per_device,
        mesh=mesh,
        in_specs=(
            P(("member", "wave"), None, None, None),
            P("wave", None, None, None),
            P(),
            P(),
            P(),
            P(),
            P(),
        ),
        out_specs=P(("member", "wave"), None, None, None),
        check_vma=False,
    )
```

profile of v0, /device:TPU:1, one launch (start us, length us, event | category | flops | bytes accessed | tf_op | source)
XLA Modules:
  0.0 301.1 jit_solution(8529033943435133871)
XLA Ops:
  4.3 11.8 %forward.1 = (bf16[8,2,32,384]{3,2,1,0:T(8,128)(2,1)S(1)}, bf16[8,2,32,384]{3,2,1,0:T(8,128)(2,1)}, bf16[8,2,32,384]{3,2,1,0:T(8,128)(2,1)}, bf16[8,2,32,384]{3,...) custom-call(s32[1]{0:T(128)} %bitcast.12.pos_ref, ...), custom_call_target="tpu_custom_call" | custom-call | tf_op jit(solution)/shard_map/forward/pallas_call | solution.py:102
  16.1 284.8 %conditional.1 = (bf16[32,2,192,256]{3,2,1,0:T(8,128)(2,1)}) conditional(s32[]{:T(128)} %convert_element_type.133, (s32[]{:T(128)}, f32[96,96]{1,0:T(8,128)S(1)}, f32[96]{0:T(128)S(1)}, f32[96]{0:T(128)S(1)}, bf16[8,2,32,384]{3,2,1,0:T(8,128)(2,1)}, /*index=5*/bf16[8,2,32,384]{3,2,1,0:T(8,128)(2,1)}, bf16[8,2,32,384]{3,2,1,0:T(8,128)(2,1)}, ...), branch_computations={%region_3.7_spmd, %region_7.11_spmd} | conditional | flops 3731156 | bytes 80234384 | solution.py:419
  16.1 5.0 %collective-permute-start.30 = (bf16[8,2,32,384]{3,2,1,0:T(8,128)(2,1)}, bf16[8,2,32,384]{3,2,1,0:T(8,128)(2,1)S(1)}, u32[]{:S(2)}, u32[]{:S(2)}) collective-permute-start(bf16[8,2,32,384]{3,2,1,0:T(8,128)(2,1)} %get-tuple-element.179), channel_id=1, source_target_pairs={{0,8},{1,9},{2,10},{3,11},{4,12},{8,0},{9,1},{10,2},{11,3},{12,4},... | collective-permute-start | bytes 1179656 | tf_op jit(solution)/shard_map/cond/branch_1_fun/ppermute | solution.py:349
  25.0 5.9 %collective-permute-start.33 = (bf16[8,2,32,384]{3,2,1,0:T(8,128)(2,1)}, bf16[8,2,32,384]{3,2,1,0:T(8,128)(2,1)S(1)}, u32[]{:S(2)}, u32[]{:S(2)}) collective-permute-start(bf16[8,2,32,384]{3,2,1,0:T(8,128)(2,1)} %get-tuple-element.182), channel_id=1, source_target_pairs={{0,9},{1,8},{2,11},{3,10},{8,1},{9,0},{10,3},{11,2},{16,25},{17,24... | collective-permute-start | bytes 1179656 | tf_op jit(solution)/shard_map/cond/branch_1_fun/ppermute | solution.py:349
  36.0 6.9 %collective-permute-done.30.rest_1_ = bf16[8,2,32,384]{3,2,1,0:T(8,128)(2,1)S(1)} collective-permute-done((bf16[8,2,32,384]{3,2,1,0:T(8,128)(2,1)}, bf16[8,2,32,384]{3,2,1,0:T(8,128)(2,1)S(1)}, u32[]{:S(2)}, u32[]{:S(2)}) %collective-permute-start.30) | collective-permute-done | bytes 393248 | tf_op jit(solution)/shard_map/cond/branch_1_fun/ppermute | solution.py:349
  49.5 14.3 %collective-permute-start.37 = (bf16[8,2,32,384]{3,2,1,0:T(8,128)(2,1)}, bf16[8,2,32,384]{3,2,1,0:T(8,128)(2,1)}, u32[]{:S(2)}, u32[]{:S(2)}) collective-permute-start(bf16[8,2,32,384]{3,2,1,0:T(8,128)(2,1)} %get-tuple-element.186), channel_id=1, source_target_pairs={{0,6},{1,7},{2,4},{3,5},{4,2},{5,3},{6,0},{7,1},{16,22},{17,23},{1... | collective-permute-start | bytes 1179656 | tf_op jit(solution)/shard_map/cond/branch_1_fun/ppermute | solution.py:349
  63.8 5.8 %collective-permute-done.33.rest_4_ = bf16[8,2,32,384]{3,2,1,0:T(8,128)(2,1)S(1)} collective-permute-done((bf16[8,2,32,384]{3,2,1,0:T(8,128)(2,1)}, bf16[8,2,32,384]{3,2,1,0:T(8,128)(2,1)S(1)}, u32[]{:S(2)}, u32[]{:S(2)}) %collective-permute-start.33) | collective-permute-done | bytes 393248 | tf_op jit(solution)/shard_map/cond/branch_1_fun/ppermute | solution.py:349
  71.7 12.5 %collective-permute-done.34.rest_5_ = bf16[8,2,32,384]{3,2,1,0:T(8,128)(2,1)S(1)} collective-permute-done((bf16[8,2,32,384]{3,2,1,0:T(8,128)(2,1)}, bf16[8,2,32,384]{3,2,1,0:T(8,128)(2,1)S(1)}, u32[]{:S(2)}, u32[]{:S(2)}) %collective-permute-start.34) | collective-permute-done | bytes 393248 | tf_op jit(solution)/shard_map/cond/branch_1_fun/ppermute | solution.py:349
  94.0 9.6 %collective-permute-done.37.rest_8_ = bf16[8,2,32,384]{3,2,1,0:T(8,128)(2,1)} collective-permute-done((bf16[8,2,32,384]{3,2,1,0:T(8,128)(2,1)}, bf16[8,2,32,384]{3,2,1,0:T(8,128)(2,1)}, u32[]{:S(2)}, u32[]{:S(2)}) %collective-permute-start.37) | collective-permute-done | bytes 393248 | tf_op jit(solution)/shard_map/cond/branch_1_fun/ppermute | solution.py:349
  114.8 8.5 %collective-permute-done.41.rest_12_ = bf16[8,2,32,384]{3,2,1,0:T(8,128)(2,1)S(1)} collective-permute-done((bf16[8,2,32,384]{3,2,1,0:T(8,128)(2,1)}, bf16[8,2,32,384]{3,2,1,0:T(8,128)(2,1)S(1)}, u32[]{:S(2)}, u32[]{:S(2)}) %collective-permute-start.41) | collective-permute-done | bytes 393248 | tf_op jit(solution)/shard_map/cond/branch_1_fun/ppermute | solution.py:349
  123.2 9.0 %collective-permute-done.42.rest_13_ = bf16[8,2,32,384]{3,2,1,0:T(8,128)(2,1)S(1)} collective-permute-done((bf16[8,2,32,384]{3,2,1,0:T(8,128)(2,1)}, bf16[8,2,32,384]{3,2,1,0:T(8,128)(2,1)S(1)}, u32[]{:S(2)}, u32[]{:S(2)}) %collective-permute-start.42) | collective-permute-done | bytes 393248 | tf_op jit(solution)/shard_map/cond/branch_1_fun/ppermute | solution.py:349
  132.3 8.4 %collective-permute-done.43.rest_14_ = bf16[8,2,32,384]{3,2,1,0:T(8,128)(2,1)S(1)} collective-permute-done((bf16[8,2,32,384]{3,2,1,0:T(8,128)(2,1)}, bf16[8,2,32,384]{3,2,1,0:T(8,128)(2,1)S(1)}, u32[]{:S(2)}, u32[]{:S(2)}) %collective-permute-start.43) | collective-permute-done | bytes 393248 | tf_op jit(solution)/shard_map/cond/branch_1_fun/ppermute | solution.py:349
  142.1 19.2 %grid.3 = (bf16[8,2,32,384]{3,2,1,0:T(8,128)(2,1)}, bf16[8,2,32,384]{3,2,1,0:T(8,128)(2,1)}, bf16[8,2,32,384]{3,2,1,0:T(8,128)(2,1)}, bf16[8,2,32,384]{3,2,1,0:T...) custom-call(s32[1]{0:T(128)} %get-tuple-element.164.pos_ref, ...), custom_call_target="tpu_custom_call" | custom-call | tf_op jit(solution)/shard_map/cond/branch_1_fun/grid/pallas_call | solution.py:207
  167.1 5.4 %collective-permute-start.48 = (bf16[8,2,32,384]{3,2,1,0:T(8,128)(2,1)}, bf16[8,2,32,384]{3,2,1,0:T(8,128)(2,1)S(1)}, u32[]{:S(2)}, u32[]{:S(2)}) collective-permute-start(bf16[8,2,32,384]{3,2,1,0:T(8,128)(2,1)} %get-tuple-element.200), channel_id=1, source_target_pairs={{0,9},{1,8},{2,11},{3,10},{8,1},{9,0},{10,3},{11,2},{16,25},{17,24... | collective-permute-start | bytes 1179656 | tf_op jit(solution)/shard_map/cond/branch_1_fun/ppermute | solution.py:349
  175.6 11.5 %collective-permute-done.45.rest_1_ = bf16[8,2,32,384]{3,2,1,0:T(8,128)(2,1)S(1)} collective-permute-done((bf16[8,2,32,384]{3,2,1,0:T(8,128)(2,1)}, bf16[8,2,32,384]{3,2,1,0:T(8,128)(2,1)S(1)}, u32[]{:S(2)}, u32[]{:S(2)}) %collective-permute-start.45) | collective-permute-done | bytes 393248 | tf_op jit(solution)/shard_map/cond/branch_1_fun/ppermute | solution.py:349
  193.4 13.7 %collective-permute-start.52 = (bf16[8,2,32,384]{3,2,1,0:T(8,128)(2,1)}, bf16[8,2,32,384]{3,2,1,0:T(8,128)(2,1)}, u32[]{:S(2)}, u32[]{:S(2)}) collective-permute-start(bf16[8,2,32,384]{3,2,1,0:T(8,128)(2,1)} %get-tuple-element.204), channel_id=1, source_target_pairs={{0,6},{1,7},{2,4},{3,5},{4,2},{5,3},{6,0},{7,1},{16,22},{17,23},{1... | collective-permute-start | bytes 1179656 | tf_op jit(solution)/shard_map/cond/branch_1_fun/ppermute | solution.py:349
  207.1 7.0 %collective-permute-done.48.rest_4_ = bf16[8,2,32,384]{3,2,1,0:T(8,128)(2,1)S(1)} collective-permute-done((bf16[8,2,32,384]{3,2,1,0:T(8,128)(2,1)}, bf16[8,2,32,384]{3,2,1,0:T(8,128)(2,1)S(1)}, u32[]{:S(2)}, u32[]{:S(2)}) %collective-permute-start.48) | collective-permute-done | bytes 393248 | tf_op jit(solution)/shard_map/cond/branch_1_fun/ppermute | solution.py:349
  215.3 7.4 %collective-permute-done.49.rest_5_ = bf16[8,2,32,384]{3,2,1,0:T(8,128)(2,1)S(1)} collective-permute-done((bf16[8,2,32,384]{3,2,1,0:T(8,128)(2,1)}, bf16[8,2,32,384]{3,2,1,0:T(8,128)(2,1)S(1)}, u32[]{:S(2)}, u32[]{:S(2)}) %collective-permute-start.49) | collective-permute-done | bytes 393248 | tf_op jit(solution)/shard_map/cond/branch_1_fun/ppermute | solution.py:349
  226.3 13.8 %all-to-all-start.1 = ((f32[16,24,128]{2,1,0:T(8,128)}), f32[16,24,128]{2,1,0:T(8,128)S(1)}, u32[]{:S(2)}, u32[]{:S(2)}) async-start(f32[16,24,128]{2,1,0:T(8,128)} %broadcast_in_dim.25), calls=%async_computation.1 | async-start | bytes 393216 | tf_op jit(solution)/shard_map/cond/branch_1_fun/all_to_all | solution.py:404
  241.5 4.4 %collective-permute-start.55 = (bf16[8,2,32,384]{3,2,1,0:T(8,128)(2,1)}, bf16[8,2,32,384]{3,2,1,0:T(8,128)(2,1)}, u32[]{:S(2)}, u32[]{:S(2)}) collective-permute-start(bf16[8,2,32,384]{3,2,1,0:T(8,128)(2,1)} %get-tuple-element.207), channel_id=1, source_target_pairs={{0,7},{1,6},{2,5},{3,4},{4,3},{5,2},{6,1},{7,0},{16,23},{17,22},{1... | collective-permute-start | bytes 1179656 | tf_op jit(solution)/shard_map/cond/branch_1_fun/ppermute | solution.py:349
  261.3 7.6 %collective-permute-done.55.rest_11_ = bf16[8,2,32,384]{3,2,1,0:T(8,128)(2,1)} collective-permute-done((bf16[8,2,32,384]{3,2,1,0:T(8,128)(2,1)}, bf16[8,2,32,384]{3,2,1,0:T(8,128)(2,1)}, u32[]{:S(2)}, u32[]{:S(2)}) %collective-permute-start.55) | collective-permute-done | bytes 393248 | tf_op jit(solution)/shard_map/cond/branch_1_fun/ppermute | solution.py:349
  268.9 8.5 %collective-permute-done.57.rest_13_ = bf16[8,2,32,384]{3,2,1,0:T(8,128)(2,1)} collective-permute-done((bf16[8,2,32,384]{3,2,1,0:T(8,128)(2,1)}, bf16[8,2,32,384]{3,2,1,0:T(8,128)(2,1)}, u32[]{:S(2)}, u32[]{:S(2)}) %collective-permute-start.57) | collective-permute-done | bytes 393248 | tf_op jit(solution)/shard_map/cond/branch_1_fun/ppermute | solution.py:349
  277.4 8.4 %collective-permute-done.58.rest_14_ = bf16[8,2,32,384]{3,2,1,0:T(8,128)(2,1)} collective-permute-done((bf16[8,2,32,384]{3,2,1,0:T(8,128)(2,1)}, bf16[8,2,32,384]{3,2,1,0:T(8,128)(2,1)}, u32[]{:S(2)}, u32[]{:S(2)}) %collective-permute-start.58) | collective-permute-done | bytes 393248 | tf_op jit(solution)/shard_map/cond/branch_1_fun/ppermute | solution.py:349
  285.9 14.8 %inverse.3 = bf16[32,2,192,256]{3,2,1,0:T(8,128)(2,1)} custom-call(s32[1]{0:T(128)} %get-tuple-element.164.pos_ref, f32[64]{0:T(128)} %reshape.629.sums_ref, bf16[32,2,192,256]{3,2,1,0:T(8,128)(2,1)} %get-tuple-element.170.spec_ref, bf16[32,2,256,256]{3,2,1,0:T(8,128)(2,1)} %get-tuple-element.171.basis_ref, s32[1,256]{1,0:T(1,128)S(1)} %get-tuple-element.172.trunc_ref, ...), custom_call_target="tpu_custom_call" | custom-call | tf_op jit(solution)/shard_map/cond/branch_1_fun/inverse/pallas_call | solution.py:303
  (164 shorter events, 79.1 us)
Async XLA Ops:
  16.1 26.7 %collective-permute-start.30 = (bf16[8,2,32,384]{3,2,1,0:T(8,128)(2,1)}, bf16[8,2,32,384]{3,2,1,0:T(8,128)(2,1)S(1)}, u32[]{:S(2)}, u32[]{:S(2)}) collective-permute-start(bf16[8,2,32,384]{3,2,1,0:T(8,128)(2,1)} %get-tuple-element.179), channel_id=1, source_target_pairs={{0,8},{1,9},{2,10},{3,11},{4,12},{8,0},{9,1},{10,2},{11,3},{12,4},... | collective-permute-start | bytes 1179656 | tf_op jit(solution)/shard_map/cond/branch_1_fun/ppermute | solution.py:349
  25.0 44.6 %collective-permute-start.33 = (bf16[8,2,32,384]{3,2,1,0:T(8,128)(2,1)}, bf16[8,2,32,384]{3,2,1,0:T(8,128)(2,1)S(1)}, u32[]{:S(2)}, u32[]{:S(2)}) collective-permute-start(bf16[8,2,32,384]{3,2,1,0:T(8,128)(2,1)} %get-tuple-element.182), channel_id=1, source_target_pairs={{0,9},{1,8},{2,11},{3,10},{8,1},{9,0},{10,3},{11,2},{16,25},{17,24... | collective-permute-start | bytes 1179656 | tf_op jit(solution)/shard_map/cond/branch_1_fun/ppermute | solution.py:349
  31.0 53.2 %collective-permute-start.34 = (bf16[8,2,32,384]{3,2,1,0:T(8,128)(2,1)}, bf16[8,2,32,384]{3,2,1,0:T(8,128)(2,1)S(1)}, u32[]{:S(2)}, u32[]{:S(2)}) collective-permute-start(bf16[8,2,32,384]{3,2,1,0:T(8,128)(2,1)} %get-tuple-element.183), channel_id=1, source_target_pairs={{0,5},{1,4},{2,7},{3,6},{4,1},{5,0},{6,3},{7,2},{16,21},{17,20},{1... | collective-permute-start | bytes 1179656 | tf_op jit(solution)/shard_map/cond/branch_1_fun/ppermute | solution.py:349
  42.9 47.9 %collective-permute-start.35 = (bf16[8,2,32,384]{3,2,1,0:T(8,128)(2,1)}, bf16[8,2,32,384]{3,2,1,0:T(8,128)(2,1)S(1)}, u32[]{:S(2)}, u32[]{:S(2)}) collective-permute-start(bf16[8,2,32,384]{3,2,1,0:T(8,128)(2,1)} %get-tuple-element.184), channel_id=1, source_target_pairs={{0,13},{1,12},{2,15},{3,14},{4,9},{5,8},{6,11},{7,10},{8,5},{9,4},... | collective-permute-start | bytes 1179656 | tf_op jit(solution)/shard_map/cond/branch_1_fun/ppermute | solution.py:349
  47.6 45.1 %collective-permute-start.36 = (bf16[8,2,32,384]{3,2,1,0:T(8,128)(2,1)}, bf16[8,2,32,384]{3,2,1,0:T(8,128)(2,1)}, u32[]{:S(2)}, u32[]{:S(2)}) collective-permute-start(bf16[8,2,32,384]{3,2,1,0:T(8,128)(2,1)} %get-tuple-element.185), channel_id=1, source_target_pairs={{0,10},{1,11},{2,8},{3,9},{8,2},{9,3},{10,0},{11,1},{16,26},{17,27... | collective-permute-start | bytes 1179656 | tf_op jit(solution)/shard_map/cond/branch_1_fun/ppermute | solution.py:349
  49.5 54.2 %collective-permute-start.37 = (bf16[8,2,32,384]{3,2,1,0:T(8,128)(2,1)}, bf16[8,2,32,384]{3,2,1,0:T(8,128)(2,1)}, u32[]{:S(2)}, u32[]{:S(2)}) collective-permute-start(bf16[8,2,32,384]{3,2,1,0:T(8,128)(2,1)} %get-tuple-element.186), channel_id=1, source_target_pairs={{0,6},{1,7},{2,4},{3,5},{4,2},{5,3},{6,0},{7,1},{16,22},{17,23},{1... | collective-permute-start | bytes 1179656 | tf_op jit(solution)/shard_map/cond/branch_1_fun/ppermute | solution.py:349
  69.6 36.0 %collective-permute-start.38 = (bf16[8,2,32,384]{3,2,1,0:T(8,128)(2,1)}, bf16[8,2,32,384]{3,2,1,0:T(8,128)(2,1)}, u32[]{:S(2)}, u32[]{:S(2)}) collective-permute-start(bf16[8,2,32,384]{3,2,1,0:T(8,128)(2,1)} %get-tuple-element.187), channel_id=1, source_target_pairs={{0,14},{1,15},{2,12},{4,10},{5,11},{6,8},{8,6},{9,7},{10,4},{12,2}... | collective-permute-start | bytes 1179656 | tf_op jit(solution)/shard_map/cond/branch_1_fun/ppermute | solution.py:349
  92.7 30.5 %collective-permute-start.41 = (bf16[8,2,32,384]{3,2,1,0:T(8,128)(2,1)}, bf16[8,2,32,384]{3,2,1,0:T(8,128)(2,1)S(1)}, u32[]{:S(2)}, u32[]{:S(2)}) collective-permute-start(bf16[8,2,32,384]{3,2,1,0:T(8,128)(2,1)} %get-tuple-element.190), channel_id=1, source_target_pairs={{0,15},{1,14},{3,12},{4,11},{5,10},{7,8},{8,7},{9,6},{11,4},{12,3}... | collective-permute-start | bytes 1179656 | tf_op jit(solution)/shard_map/cond/branch_1_fun/ppermute | solution.py:349
  103.7 28.6 %collective-permute-start.42 = (bf16[8,2,32,384]{3,2,1,0:T(8,128)(2,1)}, bf16[8,2,32,384]{3,2,1,0:T(8,128)(2,1)S(1)}, u32[]{:S(2)}, u32[]{:S(2)}) collective-permute-start(bf16[8,2,32,384]{3,2,1,0:T(8,128)(2,1)} %get-tuple-element.191), channel_id=1, source_target_pairs={{0,3},{1,2},{2,1},{3,0},{4,7},{5,6},{6,5},{7,4},{16,19},{17,18},{1... | collective-permute-start | bytes 1179656 | tf_op jit(solution)/shard_map/cond/branch_1_fun/ppermute | solution.py:349
  105.6 35.1 %collective-permute-start.43 = (bf16[8,2,32,384]{3,2,1,0:T(8,128)(2,1)}, bf16[8,2,32,384]{3,2,1,0:T(8,128)(2,1)S(1)}, u32[]{:S(2)}, u32[]{:S(2)}) collective-permute-start(bf16[8,2,32,384]{3,2,1,0:T(8,128)(2,1)} %get-tuple-element.192), channel_id=1, source_target_pairs={{0,2},{1,3},{2,0},{3,1},{4,6},{5,7},{6,4},{7,5},{16,18},{17,19},{1... | collective-permute-start | bytes 1179656 | tf_op jit(solution)/shard_map/cond/branch_1_fun/ppermute | solution.py:349
  109.5 31.2 %collective-permute-start.44 = (bf16[8,2,32,384]{3,2,1,0:T(8,128)(2,1)}, bf16[8,2,32,384]{3,2,1,0:T(8,128)(2,1)S(1)}, u32[]{:S(2)}, u32[]{:S(2)}) collective-permute-start(bf16[8,2,32,384]{3,2,1,0:T(8,128)(2,1)} %get-tuple-element.193), channel_id=1, source_target_pairs={{0,1},{1,0},{2,3},{3,2},{4,5},{5,4},{6,7},{7,6},{16,17},{17,16},{1... | collective-permute-start | bytes 1179656 | tf_op jit(solution)/shard_map/cond/branch_1_fun/ppermute | solution.py:349
  163.2 28.2 %collective-permute-start.46 = (bf16[8,2,32,384]{3,2,1,0:T(8,128)(2,1)}, bf16[8,2,32,384]{3,2,1,0:T(8,128)(2,1)S(1)}, u32[]{:S(2)}, u32[]{:S(2)}) collective-permute-start(bf16[8,2,32,384]{3,2,1,0:T(8,128)(2,1)} %get-tuple-element.198), channel_id=1, source_target_pairs={{0,4},{1,5},{2,6},{3,7},{4,0},{5,1},{6,2},{7,3},{16,20},{17,21},{1... | collective-permute-start | bytes 1179656 | tf_op jit(solution)/shard_map/cond/branch_1_fun/ppermute | solution.py:349
  165.1 28.2 %collective-permute-start.47 = (bf16[8,2,32,384]{3,2,1,0:T(8,128)(2,1)}, bf16[8,2,32,384]{3,2,1,0:T(8,128)(2,1)S(1)}, u32[]{:S(2)}, u32[]{:S(2)}) collective-permute-start(bf16[8,2,32,384]{3,2,1,0:T(8,128)(2,1)} %get-tuple-element.199), channel_id=1, source_target_pairs={{0,12},{1,13},{2,14},{4,8},{5,9},{6,10},{8,4},{9,5},{10,6},{12,0},... | collective-permute-start | bytes 1179656 | tf_op jit(solution)/shard_map/cond/branch_1_fun/ppermute | solution.py:349
  167.1 47.0 %collective-permute-start.48 = (bf16[8,2,32,384]{3,2,1,0:T(8,128)(2,1)}, bf16[8,2,32,384]{3,2,1,0:T(8,128)(2,1)S(1)}, u32[]{:S(2)}, u32[]{:S(2)}) collective-permute-start(bf16[8,2,32,384]{3,2,1,0:T(8,128)(2,1)} %get-tuple-element.200), channel_id=1, source_target_pairs={{0,9},{1,8},{2,11},{3,10},{8,1},{9,0},{10,3},{11,2},{16,25},{17,24... | collective-permute-start | bytes 1179656 | tf_op jit(solution)/shard_map/cond/branch_1_fun/ppermute | solution.py:349
  172.5 50.2 %collective-permute-start.49 = (bf16[8,2,32,384]{3,2,1,0:T(8,128)(2,1)}, bf16[8,2,32,384]{3,2,1,0:T(8,128)(2,1)S(1)}, u32[]{:S(2)}, u32[]{:S(2)}) collective-permute-start(bf16[8,2,32,384]{3,2,1,0:T(8,128)(2,1)} %get-tuple-element.201), channel_id=1, source_target_pairs={{0,5},{1,4},{2,7},{3,6},{4,1},{5,0},{6,3},{7,2},{16,21},{17,20},{1... | collective-permute-start | bytes 1179656 | tf_op jit(solution)/shard_map/cond/branch_1_fun/ppermute | solution.py:349
  187.2 54.3 %collective-permute-start.50 = (bf16[8,2,32,384]{3,2,1,0:T(8,128)(2,1)}, bf16[8,2,32,384]{3,2,1,0:T(8,128)(2,1)S(1)}, u32[]{:S(2)}, u32[]{:S(2)}) collective-permute-start(bf16[8,2,32,384]{3,2,1,0:T(8,128)(2,1)} %get-tuple-element.202), channel_id=1, source_target_pairs={{0,13},{1,12},{2,15},{3,14},{4,9},{5,8},{6,11},{7,10},{8,5},{9,4},... | collective-permute-start | bytes 1179656 | tf_op jit(solution)/shard_map/cond/branch_1_fun/ppermute | solution.py:349
  191.4 54.5 %collective-permute-start.51 = (bf16[8,2,32,384]{3,2,1,0:T(8,128)(2,1)}, bf16[8,2,32,384]{3,2,1,0:T(8,128)(2,1)S(1)}, u32[]{:S(2)}, u32[]{:S(2)}) collective-permute-start(bf16[8,2,32,384]{3,2,1,0:T(8,128)(2,1)} %get-tuple-element.203), channel_id=1, source_target_pairs={{0,10},{1,11},{2,8},{3,9},{8,2},{9,3},{10,0},{11,1},{16,26},{17,27... | collective-permute-start | bytes 1179656 | tf_op jit(solution)/shard_map/cond/branch_1_fun/ppermute | solution.py:349
  193.4 57.6 %collective-permute-start.52 = (bf16[8,2,32,384]{3,2,1,0:T(8,128)(2,1)}, bf16[8,2,32,384]{3,2,1,0:T(8,128)(2,1)}, u32[]{:S(2)}, u32[]{:S(2)}) collective-permute-start(bf16[8,2,32,384]{3,2,1,0:T(8,128)(2,1)} %get-tuple-element.204), channel_id=1, source_target_pairs={{0,6},{1,7},{2,4},{3,5},{4,2},{5,3},{6,0},{7,1},{16,22},{17,23},{1... | collective-permute-start | bytes 1179656 | tf_op jit(solution)/shard_map/cond/branch_1_fun/ppermute | solution.py:349
  214.0 38.9 %collective-permute-start.53 = (bf16[8,2,32,384]{3,2,1,0:T(8,128)(2,1)}, bf16[8,2,32,384]{3,2,1,0:T(8,128)(2,1)}, u32[]{:S(2)}, u32[]{:S(2)}) collective-permute-start(bf16[8,2,32,384]{3,2,1,0:T(8,128)(2,1)} %get-tuple-element.205), channel_id=1, source_target_pairs={{0,14},{2,12},{3,13},{4,10},{6,8},{7,9},{8,6},{10,4},{11,5},{12,2}... | collective-permute-start | bytes 1179656 | tf_op jit(solution)/shard_map/cond/branch_1_fun/ppermute | solution.py:349
  222.7 34.1 %collective-permute-start.54 = (bf16[8,2,32,384]{3,2,1,0:T(8,128)(2,1)}, bf16[8,2,32,384]{3,2,1,0:T(8,128)(2,1)}, u32[]{:S(2)}, u32[]{:S(2)}) collective-permute-start(bf16[8,2,32,384]{3,2,1,0:T(8,128)(2,1)} %get-tuple-element.206), channel_id=1, source_target_pairs={{0,11},{1,10},{2,9},{3,8},{8,3},{9,2},{10,1},{11,0},{16,27},{17,26... | collective-permute-start | bytes 1179656 | tf_op jit(solution)/shard_map/cond/branch_1_fun/ppermute | solution.py:349
  226.3 33.5 %all-to-all-start.1 = ((f32[16,24,128]{2,1,0:T(8,128)}), f32[16,24,128]{2,1,0:T(8,128)S(1)}, u32[]{:S(2)}, u32[]{:S(2)}) async-start(f32[16,24,128]{2,1,0:T(8,128)} %broadcast_in_dim.25), calls=%async_computation.1 | async-start | bytes 393216 | tf_op jit(solution)/shard_map/cond/branch_1_fun/all_to_all | solution.py:404
  241.5 27.4 %collective-permute-start.55 = (bf16[8,2,32,384]{3,2,1,0:T(8,128)(2,1)}, bf16[8,2,32,384]{3,2,1,0:T(8,128)(2,1)}, u32[]{:S(2)}, u32[]{:S(2)}) collective-permute-start(bf16[8,2,32,384]{3,2,1,0:T(8,128)(2,1)} %get-tuple-element.207), channel_id=1, source_target_pairs={{0,7},{1,6},{2,5},{3,4},{4,3},{5,2},{6,1},{7,0},{16,23},{17,22},{1... | collective-permute-start | bytes 1179656 | tf_op jit(solution)/shard_map/cond/branch_1_fun/ppermute | solution.py:349
  252.9 32.9 %collective-permute-start.58 = (bf16[8,2,32,384]{3,2,1,0:T(8,128)(2,1)}, bf16[8,2,32,384]{3,2,1,0:T(8,128)(2,1)}, u32[]{:S(2)}, u32[]{:S(2)}) collective-permute-start(bf16[8,2,32,384]{3,2,1,0:T(8,128)(2,1)} %get-tuple-element.210), channel_id=1, source_target_pairs={{0,2},{1,3},{2,0},{3,1},{4,6},{5,7},{6,4},{7,5},{16,18},{17,19},{1... | collective-permute-start | bytes 1179656 | tf_op jit(solution)/shard_map/cond/branch_1_fun/ppermute | solution.py:349
  256.8 29.1 %collective-permute-start.59 = (bf16[8,2,32,384]{3,2,1,0:T(8,128)(2,1)}, bf16[8,2,32,384]{3,2,1,0:T(8,128)(2,1)}, u32[]{:S(2)}, u32[]{:S(2)}) collective-permute-start(bf16[8,2,32,384]{3,2,1,0:T(8,128)(2,1)} %get-tuple-element.211), channel_id=1, source_target_pairs={{0,1},{1,0},{2,3},{3,2},{4,5},{5,4},{6,7},{7,6},{16,17},{17,16},{1... | collective-permute-start | bytes 1179656 | tf_op jit(solution)/shard_map/cond/branch_1_fun/ppermute | solution.py:349
  (32 other events, 1595.4 us)
where the time goes:
time: 303 us; the launch traced here: 301 us
  waiting for transfers between devices  125 us (41%)
  starting transfers between devices  108 us (36%)
  Pallas kernels  45.7 us (15%)
  local copies, waits for them, and re-layouts  10.4 us (3%)
  other arithmetic  8.81 us (3%)
    ppermute x30, waiting for transfers between devices, exchange(): got.append(lax.ppermute(array, 'wave', pairs))  125 us
    ppermute x30, starting transfers between devices, exchange(): got.append(lax.ppermute(array, 'wave', pairs))  94.4 us
    pallas_call x1, Pallas kernels, on_grid(): pl.pallas_call(functools.partial(grid_kernel, devices, waves, unroll), gr...  19.2 us
    pallas_call x1, Pallas kernels, inverse(): pl.pallas_call(functools.partial(inverse_kernel, devices, group, waves, u...  14.8 us
    all_to_all x1, starting transfers between devices, finish(): lax.all_to_all(sent, 'wave', split_axis=0, concat_axis=0, tiled=True)  13.8 us
    pallas_call x1, Pallas kernels, forward(): pl.pallas_call(functools.partial(forward_kernel, devices, group, waves),...  11.8 us
  transfers between devices with their start and end apart: 31, of which 17 were waited for; matrix products, arithmetic and copies ran while one was open for 5% of the time, Pallas kernels for 0%

commit v1 on v0

--- a/solution.py
+++ b/solution.py
@@ -3,6 +3,7 @@
 
 import jax
 import jax.numpy as jnp
+import numpy as np
 from jax import lax
 from jax.experimental import pallas as pl
 from jax.experimental.pallas import tpu as pltpu
@@ -32,13 +33,11 @@
 def latitude_order(half_lats, devices):
     rows = half_lats // devices
     pairs = rows // 2
-    lane = jnp.arange(half_lats, dtype=jnp.int32)
+    lane = np.arange(half_lats)
     half = lane // (half_lats // 2)
     owner = lane % (half_lats // 2) // pairs
-    pair = lane % pairs
-    groups = jnp.array(owned_groups(devices), dtype=jnp.int32)
-    group = jnp.sum(jnp.where(owner[:, None] == jnp.arange(devices), groups[None, :], 0), axis=1)
-    return group * rows + half * pairs + pair
+    group = np.array(owned_groups(devices))[owner]
+    return (group * rows + half * pairs + lane % pairs).astype(np.int32)
 
 
 def exchange_order(devices):
@@ -342,11 +341,21 @@
     return cos.reshape(size, size).astype(BF16), (-sin).reshape(size, size).astype(BF16)
 
 
-def exchange(arrays, devices, needed):
+def exchange(arrays, devices, needed, relay=False):
+    quarter = devices // 4
+    hop = quarter // 2
+    far = 3 * quarter + hop
+    handed = [d for d in range(devices) if relay and hop and not d & hop and needed(d, d ^ far)]
+    order = exchange_order(devices)
+    if handed:
+        moved = lax.ppermute(arrays[order.index(far)], "wave", [(d, d ^ hop) for d in handed])
+        moved = lax.ppermute(moved, "wave", [(d ^ hop, d ^ far) for d in handed])
     got = [arrays[0]]
-    for array, s in list(zip(arrays, exchange_order(devices)))[1:]:
-        pairs = [(i, i ^ s) for i in range(devices) if needed(i, i ^ s)]
-        got.append(lax.ppermute(array, "wave", pairs))
+    for array, s in list(zip(arrays, order))[1:]:
+        skip = handed if s == far else []
+        pairs = [(i, i ^ s) for i in range(devices) if needed(i, i ^ s) and i not in skip]
+        array = lax.ppermute(array, "wave", pairs)
+        got.append(array + moved if skip else array)
     return got
 
 
@@ -370,8 +379,7 @@
 
     groups = owned_groups(devices)
     reach = [min(devices, g + 1 + max(1, devices // 16)) for g in range(devices)]
-    top = jnp.max(trunc.reshape(devices, rows), axis=1)
-    fits = jnp.all(top <= waves * jnp.array(reach, dtype=jnp.int32))
+    fits = jnp.all(trunc <= jnp.array(np.repeat(waves * np.array(reach, np.int32), rows)))
 
     def finish(sparse, blocks):
         def there(source, owner):
@@ -393,7 +401,7 @@
         held = jnp.swapaxes(jnp.stack([held[g] for g in groups]), 1, 2)
         held = held.reshape(devices * pairs, 2, 1, 1) / (2.0 * jnp.sum(quad_weights))
 
-        got = exchange(blocks, devices, there)
+        got = exchange(blocks, devices, there, relay=sparse)
         *parts, means = on_grid(
             pos, cosine, sine, middle, mix, coef, got, STEPS if sparse else 1
         )

time: 303 us -> 301 us (level)
  waiting for transfers between devices: 125 us -> 110 us
  starting transfers between devices: 108 us -> 117 us
  other arithmetic: 8.81 us -> 12 us
    ppermute x30 -> x32, waiting for transfers between devices: 125 us -> 110 us  [the longest x30 110 us: exchange(): array = lax.ppermute(array, 'wave', pairs)]
    ppermute x30 -> x32, starting transfers between devices: 94.4 us -> 107 us  [the longest x30 88.6 us: exchange(): array = lax.ppermute(array, 'wave', pairs)]
    all_to_all x1, starting transfers between devices: 13.8 us -> 10.2 us  [finish(): lax.all_to_all(sent, 'wave', split_axis=0, concat_axis=0, tiled=True)]
  transfers between devices with their start and end apart: 31 -> 33, of which waited for: 17 -> 16; matrix products, arithmetic and copies ran while one was open for 5% -> 7% of each run, Pallas kernels for 0% -> 0%
where the time goes in v1:
time: 301 us; the launch traced here: 299 us
  starting transfers between devices  117 us (39%)
  waiting for transfers between devices  110 us (37%)
  Pallas kernels  45.7 us (15%)
  local copies, waits for them, and re-layouts  12.3 us (4%)
  other arithmetic  12 us (4%)
    ppermute x30, waiting for transfers between devices, exchange(): array = lax.ppermute(array, 'wave', pairs)  110 us
    ppermute x30, starting transfers between devices, exchange(): array = lax.ppermute(array, 'wave', pairs)  88.6 us
    pallas_call x1, Pallas kernels, on_grid(): pl.pallas_call(functools.partial(grid_kernel, devices, waves, unroll), gr...  19.3 us
    ppermute x1, starting transfers between devices, exchange(): lax.ppermute(arrays[order.index(far)], 'wave', [(d, d ^ hop) for d in han...  16.8 us
    pallas_call x1, Pallas kernels, inverse(): pl.pallas_call(functools.partial(inverse_kernel, devices, group, waves, u...  14.8 us
    pallas_call x1, Pallas kernels, forward(): pl.pallas_call(functools.partial(forward_kernel, devices, group, waves),...  11.7 us
    all_to_all x1, starting transfers between devices, finish(): lax.all_to_all(sent, 'wave', split_axis=0, concat_axis=0, tiled=True)  10.2 us
  transfers between devices with their start and end apart: 33, of which 16 were waited for; matrix products, arithmetic and copies ran while one was open for 7% of the time, Pallas kernels for 0%

profile of v1, /device:TPU:1, one launch (start us, length us, event | category | flops | bytes accessed | tf_op | source)
XLA Modules:
  0.0 299.1 jit_solution(441099614976597251)
XLA Ops:
  3.5 11.7 %forward.1 = (bf16[8,2,32,384]{3,2,1,0:T(8,128)(2,1)S(1)}, bf16[8,2,32,384]{3,2,1,0:T(8,128)(2,1)}, bf16[8,2,32,384]{3,2,1,0:T(8,128)(2,1)}, bf16[8,2,32,384]{3,...) custom-call(s32[1]{0:T(128)} %bitcast.12.pos_ref, ...), custom_call_target="tpu_custom_call" | custom-call | tf_op jit(solution)/shard_map/forward/pallas_call | solution.py:101
  15.2 283.7 %conditional.1 = (bf16[32,2,192,256]{3,2,1,0:T(8,128)(2,1)}) conditional(s32[]{:T(128)} %convert_element_type.133, (s32[]{:T(128)}, f32[96,96]{1,0:T(8,128)S(1)}, f32[96]{0:T(128)S(1)}, f32[96]{0:T(128)S(1)}, bf16[8,2,32,384]{3,2,1,0:T(8,128)(2,1)}, /*index=5*/bf16[8,2,32,384]{3,2,1,0:T(8,128)(2,1)}, bf16[8,2,32,384]{3,2,1,0:T(8,128)(2,1)}, ...), branch_computations={%region_1.5_spmd, %region_5.9_spmd} | conditional | flops 3927764 | bytes 84566768 | solution.py:427
  15.2 5.0 %collective-permute-start.30 = (bf16[8,2,32,384]{3,2,1,0:T(8,128)(2,1)}, bf16[8,2,32,384]{3,2,1,0:T(8,128)(2,1)S(1)}, u32[]{:S(2)}, u32[]{:S(2)}) collective-permute-start(bf16[8,2,32,384]{3,2,1,0:T(8,128)(2,1)} %get-tuple-element.179), channel_id=1, source_target_pairs={{0,8},{1,9},{2,10},{3,11},{4,12},{8,0},{9,1},{10,2},{11,3},{12,4},... | collective-permute-start | bytes 1179656 | tf_op jit(solution)/shard_map/cond/branch_1_fun/ppermute | solution.py:357
  24.1 5.9 %collective-permute-start.33 = (bf16[8,2,32,384]{3,2,1,0:T(8,128)(2,1)}, bf16[8,2,32,384]{3,2,1,0:T(8,128)(2,1)S(1)}, u32[]{:S(2)}, u32[]{:S(2)}) collective-permute-start(bf16[8,2,32,384]{3,2,1,0:T(8,128)(2,1)} %get-tuple-element.182), channel_id=1, source_target_pairs={{0,9},{1,8},{2,11},{3,10},{8,1},{9,0},{10,3},{11,2},{16,25},{17,24... | collective-permute-start | bytes 1179656 | tf_op jit(solution)/shard_map/cond/branch_1_fun/ppermute | solution.py:357
  34.9 7.0 %collective-permute-done.30.rest_1_ = bf16[8,2,32,384]{3,2,1,0:T(8,128)(2,1)S(1)} collective-permute-done((bf16[8,2,32,384]{3,2,1,0:T(8,128)(2,1)}, bf16[8,2,32,384]{3,2,1,0:T(8,128)(2,1)S(1)}, u32[]{:S(2)}, u32[]{:S(2)}) %collective-permute-start.30) | collective-permute-done | bytes 393248 | tf_op jit(solution)/shard_map/cond/branch_1_fun/ppermute | solution.py:357
  46.7 16.8 %collective-permute-start.39 = (bf16[8,2,32,384]{3,2,1,0:T(8,128)(2,1)}, bf16[8,2,32,384]{3,2,1,0:T(8,128)(2,1)}, u32[]{:S(2)}, u32[]{:S(2)}) collective-permute-start(bf16[8,2,32,384]{3,2,1,0:T(8,128)(2,1)} %get-tuple-element.187), channel_id=1, source_target_pairs={{0,2},{1,3},{4,6},{5,7},{8,10},{9,11},{12,14},{13,15},{16,18},{17,... | collective-permute-start | bytes 1179656 | tf_op jit(solution)/shard_map/cond/branch_1_fun/ppermute | solution.py:351
  86.4 5.6 %collective-permute-start.42 = (bf16[8,2,32,384]{3,2,1,0:T(8,128)(2,1)}, bf16[8,2,32,384]{3,2,1,0:T(8,128)(2,1)S(1)}, u32[]{:S(2)}, u32[]{:S(2)}) collective-permute-start(bf16[8,2,32,384]{3,2,1,0:T(8,128)(2,1)} %get-tuple-element.189), channel_id=1, source_target_pairs={{0,7},{1,6},{2,5},{3,4},{4,3},{5,2},{6,1},{7,0},{16,23},{17,22},{1... | collective-permute-start | bytes 1179656 | tf_op jit(solution)/shard_map/cond/branch_1_fun/ppermute | solution.py:357
  92.0 19.8 %collective-permute-done.37.rest_8_ = bf16[8,2,32,384]{3,2,1,0:T(8,128)(2,1)} collective-permute-done((bf16[8,2,32,384]{3,2,1,0:T(8,128)(2,1)}, bf16[8,2,32,384]{3,2,1,0:T(8,128)(2,1)}, u32[]{:S(2)}, u32[]{:S(2)}) %collective-permute-start.37) | collective-permute-done | bytes 393248 | tf_op jit(solution)/shard_map/cond/branch_1_fun/ppermute | solution.py:357
  115.1 4.2 %collective-permute-start.45 = (bf16[8,2,32,384]{3,2,1,0:T(8,128)(2,1)}, bf16[8,2,32,384]{3,2,1,0:T(8,128)(2,1)S(1)}, u32[]{:S(2)}, u32[]{:S(2)}) collective-permute-start(bf16[8,2,32,384]{3,2,1,0:T(8,128)(2,1)} %get-tuple-element.192), channel_id=1, source_target_pairs={{0,2},{1,3},{2,0},{3,1},{4,6},{5,7},{6,4},{7,5},{16,18},{17,19},{1... | collective-permute-start | bytes 1179656 | tf_op jit(solution)/shard_map/cond/branch_1_fun/ppermute | solution.py:357
  124.4 8.5 %collective-permute-done.44.rest_13_ = bf16[8,2,32,384]{3,2,1,0:T(8,128)(2,1)S(1)} collective-permute-done((bf16[8,2,32,384]{3,2,1,0:T(8,128)(2,1)}, bf16[8,2,32,384]{3,2,1,0:T(8,128)(2,1)S(1)}, u32[]{:S(2)}, u32[]{:S(2)}) %collective-permute-start.44) | collective-permute-done | bytes 393248 | tf_op jit(solution)/shard_map/cond/branch_1_fun/ppermute | solution.py:357
  132.9 8.4 %collective-permute-done.45.rest_14_ = bf16[8,2,32,384]{3,2,1,0:T(8,128)(2,1)S(1)} collective-permute-done((bf16[8,2,32,384]{3,2,1,0:T(8,128)(2,1)}, bf16[8,2,32,384]{3,2,1,0:T(8,128)(2,1)S(1)}, u32[]{:S(2)}, u32[]{:S(2)}) %collective-permute-start.45) | collective-permute-done | bytes 393248 | tf_op jit(solution)/shard_map/cond/branch_1_fun/ppermute | solution.py:357
  142.7 19.3 %grid.3 = (bf16[8,2,32,384]{3,2,1,0:T(8,128)(2,1)}, bf16[8,2,32,384]{3,2,1,0:T(8,128)(2,1)}, bf16[8,2,32,384]{3,2,1,0:T(8,128)(2,1)}, bf16[8,2,32,384]{3,2,1,0:T...) custom-call(s32[1]{0:T(128)} %get-tuple-element.164.pos_ref, ...), custom_call_target="tpu_custom_call" | custom-call | tf_op jit(solution)/shard_map/cond/branch_1_fun/grid/pallas_call | solution.py:206
  167.8 5.4 %collective-permute-start.50 = (bf16[8,2,32,384]{3,2,1,0:T(8,128)(2,1)}, bf16[8,2,32,384]{3,2,1,0:T(8,128)(2,1)S(1)}, u32[]{:S(2)}, u32[]{:S(2)}) collective-permute-start(bf16[8,2,32,384]{3,2,1,0:T(8,128)(2,1)} %get-tuple-element.200), channel_id=1, source_target_pairs={{0,9},{1,8},{2,11},{3,10},{8,1},{9,0},{10,3},{11,2},{16,25},{17,24... | collective-permute-start | bytes 1179656 | tf_op jit(solution)/shard_map/cond/branch_1_fun/ppermute | solution.py:357
  176.3 12.2 %collective-permute-done.47.rest_1_ = bf16[8,2,32,384]{3,2,1,0:T(8,128)(2,1)S(1)} collective-permute-done((bf16[8,2,32,384]{3,2,1,0:T(8,128)(2,1)}, bf16[8,2,32,384]{3,2,1,0:T(8,128)(2,1)S(1)}, u32[]{:S(2)}, u32[]{:S(2)}) %collective-permute-start.47) | collective-permute-done | bytes 393248 | tf_op jit(solution)/shard_map/cond/branch_1_fun/ppermute | solution.py:357
  188.5 4.5 %collective-permute-done.48.rest_2_ = bf16[8,2,32,384]{3,2,1,0:T(8,128)(2,1)S(1)} collective-permute-done((bf16[8,2,32,384]{3,2,1,0:T(8,128)(2,1)}, bf16[8,2,32,384]{3,2,1,0:T(8,128)(2,1)S(1)}, u32[]{:S(2)}, u32[]{:S(2)}) %collective-permute-start.48) | collective-permute-done | bytes 393248 | tf_op jit(solution)/shard_map/cond/branch_1_fun/ppermute | solution.py:357
  195.0 10.2 %collective-permute-start.54 = (bf16[8,2,32,384]{3,2,1,0:T(8,128)(2,1)}, bf16[8,2,32,384]{3,2,1,0:T(8,128)(2,1)}, u32[]{:S(2)}, u32[]{:S(2)}) collective-permute-start(bf16[8,2,32,384]{3,2,1,0:T(8,128)(2,1)} %get-tuple-element.204), channel_id=1, source_target_pairs={{0,6},{1,7},{2,4},{3,5},{4,2},{5,3},{6,0},{7,1},{16,22},{17,23},{1... | collective-permute-start | bytes 1179656 | tf_op jit(solution)/shard_map/cond/branch_1_fun/ppermute | solution.py:357
  205.2 8.8 %collective-permute-done.50.rest_4_ = bf16[8,2,32,384]{3,2,1,0:T(8,128)(2,1)S(1)} collective-permute-done((bf16[8,2,32,384]{3,2,1,0:T(8,128)(2,1)}, bf16[8,2,32,384]{3,2,1,0:T(8,128)(2,1)S(1)}, u32[]{:S(2)}, u32[]{:S(2)}) %collective-permute-start.50) | collective-permute-done | bytes 393248 | tf_op jit(solution)/shard_map/cond/branch_1_fun/ppermute | solution.py:357
  215.3 9.1 %collective-permute-done.51.rest_5_ = bf16[8,2,32,384]{3,2,1,0:T(8,128)(2,1)S(1)} collective-permute-done((bf16[8,2,32,384]{3,2,1,0:T(8,128)(2,1)}, bf16[8,2,32,384]{3,2,1,0:T(8,128)(2,1)S(1)}, u32[]{:S(2)}, u32[]{:S(2)}) %collective-permute-start.51) | collective-permute-done | bytes 393248 | tf_op jit(solution)/shard_map/cond/branch_1_fun/ppermute | solution.py:357
  228.0 10.2 %all-to-all-start.1 = ((f32[16,24,128]{2,1,0:T(8,128)}), f32[16,24,128]{2,1,0:T(8,128)S(1)}, u32[]{:S(2)}, u32[]{:S(2)}) async-start(f32[16,24,128]{2,1,0:T(8,128)} %broadcast_in_dim.15), calls=%async_computation.1 | async-start | bytes 393216 | tf_op jit(solution)/shard_map/cond/branch_1_fun/all_to_all | solution.py:412
  239.3 4.4 %collective-permute-start.57 = (bf16[8,2,32,384]{3,2,1,0:T(8,128)(2,1)}, bf16[8,2,32,384]{3,2,1,0:T(8,128)(2,1)}, u32[]{:S(2)}, u32[]{:S(2)}) collective-permute-start(bf16[8,2,32,384]{3,2,1,0:T(8,128)(2,1)} %get-tuple-element.207), channel_id=1, source_target_pairs={{0,7},{1,6},{2,5},{3,4},{4,3},{5,2},{6,1},{7,0},{16,23},{17,22},{1... | collective-permute-start | bytes 1179656 | tf_op jit(solution)/shard_map/cond/branch_1_fun/ppermute | solution.py:357
  249.0 10.3 %collective-permute-start.59 = (bf16[8,2,32,384]{3,2,1,0:T(8,128)(2,1)}, bf16[8,2,32,384]{3,2,1,0:T(8,128)(2,1)}, u32[]{:S(2)}, u32[]{:S(2)}) collective-permute-start(bf16[8,2,32,384]{3,2,1,0:T(8,128)(2,1)} %get-tuple-element.209), channel_id=1, source_target_pairs={{0,3},{1,2},{2,1},{3,0},{4,7},{5,6},{6,5},{7,4},{16,19},{17,18},{1... | collective-permute-start | bytes 1179656 | tf_op jit(solution)/shard_map/cond/branch_1_fun/ppermute | solution.py:357
  267.0 8.5 %collective-permute-done.59.rest_13_ = bf16[8,2,32,384]{3,2,1,0:T(8,128)(2,1)} collective-permute-done((bf16[8,2,32,384]{3,2,1,0:T(8,128)(2,1)}, bf16[8,2,32,384]{3,2,1,0:T(8,128)(2,1)}, u32[]{:S(2)}, u32[]{:S(2)}) %collective-permute-start.59) | collective-permute-done | bytes 393248 | tf_op jit(solution)/shard_map/cond/branch_1_fun/ppermute | solution.py:357
  275.4 8.4 %collective-permute-done.60.rest_14_ = bf16[8,2,32,384]{3,2,1,0:T(8,128)(2,1)} collective-permute-done((bf16[8,2,32,384]{3,2,1,0:T(8,128)(2,1)}, bf16[8,2,32,384]{3,2,1,0:T(8,128)(2,1)}, u32[]{:S(2)}, u32[]{:S(2)}) %collective-permute-start.60) | collective-permute-done | bytes 393248 | tf_op jit(solution)/shard_map/cond/branch_1_fun/ppermute | solution.py:357
  283.9 14.8 %inverse.3 = bf16[32,2,192,256]{3,2,1,0:T(8,128)(2,1)} custom-call(s32[1]{0:T(128)} %get-tuple-element.164.pos_ref, f32[64]{0:T(128)} %reshape.550.sums_ref, bf16[32,2,192,256]{3,2,1,0:T(8,128)(2,1)} %get-tuple-element.170.spec_ref, bf16[32,2,256,256]{3,2,1,0:T(8,128)(2,1)} %get-tuple-element.171.basis_ref, s32[1,256]{1,0:T(1,128)S(1)} %get-tuple-element.172.trunc_ref, ...), custom_call_target="tpu_custom_call" | custom-call | tf_op jit(solution)/shard_map/cond/branch_1_fun/inverse/pallas_call | solution.py:302
  (170 shorter events, 77.7 us)
Async XLA Ops:
  15.2 26.7 %collective-permute-start.30 = (bf16[8,2,32,384]{3,2,1,0:T(8,128)(2,1)}, bf16[8,2,32,384]{3,2,1,0:T(8,128)(2,1)S(1)}, u32[]{:S(2)}, u32[]{:S(2)}) collective-permute-start(bf16[8,2,32,384]{3,2,1,0:T(8,128)(2,1)} %get-tuple-element.179), channel_id=1, source_target_pairs={{0,8},{1,9},{2,10},{3,11},{4,12},{8,0},{9,1},{10,2},{11,3},{12,4},... | collective-permute-start | bytes 1179656 | tf_op jit(solution)/shard_map/cond/branch_1_fun/ppermute | solution.py:357
  22.2 42.4 %collective-permute-start.32 = (bf16[8,2,32,384]{3,2,1,0:T(8,128)(2,1)}, bf16[8,2,32,384]{3,2,1,0:T(8,128)(2,1)S(1)}, u32[]{:S(2)}, u32[]{:S(2)}) collective-permute-start(bf16[8,2,32,384]{3,2,1,0:T(8,128)(2,1)} %get-tuple-element.181), channel_id=1, source_target_pairs={{0,12},{1,13},{2,14},{4,8},{5,9},{6,10},{8,4},{9,5},{10,6},{12,0},... | collective-permute-start | bytes 1179656 | tf_op jit(solution)/shard_map/cond/branch_1_fun/ppermute | solution.py:357
  24.1 44.6 %collective-permute-start.33 = (bf16[8,2,32,384]{3,2,1,0:T(8,128)(2,1)}, bf16[8,2,32,384]{3,2,1,0:T(8,128)(2,1)S(1)}, u32[]{:S(2)}, u32[]{:S(2)}) collective-permute-start(bf16[8,2,32,384]{3,2,1,0:T(8,128)(2,1)} %get-tuple-element.182), channel_id=1, source_target_pairs={{0,9},{1,8},{2,11},{3,10},{8,1},{9,0},{10,3},{11,2},{16,25},{17,24... | collective-permute-start | bytes 1179656 | tf_op jit(solution)/shard_map/cond/branch_1_fun/ppermute | solution.py:357
  30.1 43.0 %collective-permute-start.34 = (bf16[8,2,32,384]{3,2,1,0:T(8,128)(2,1)}, bf16[8,2,32,384]{3,2,1,0:T(8,128)(2,1)S(1)}, u32[]{:S(2)}, u32[]{:S(2)}) collective-permute-start(bf16[8,2,32,384]{3,2,1,0:T(8,128)(2,1)} %get-tuple-element.183), channel_id=1, source_target_pairs={{0,5},{1,4},{2,7},{3,6},{4,1},{5,0},{6,3},{7,2},{16,21},{17,20},{1... | collective-permute-start | bytes 1179656 | tf_op jit(solution)/shard_map/cond/branch_1_fun/ppermute | solution.py:357
  42.0 33.0 %collective-permute-start.35 = (bf16[8,2,32,384]{3,2,1,0:T(8,128)(2,1)}, bf16[8,2,32,384]{3,2,1,0:T(8,128)(2,1)S(1)}, u32[]{:S(2)}, u32[]{:S(2)}) collective-permute-start(bf16[8,2,32,384]{3,2,1,0:T(8,128)(2,1)} %get-tuple-element.184), channel_id=1, source_target_pairs={{0,13},{1,12},{2,15},{3,14},{4,9},{5,8},{6,11},{7,10},{8,5},{9,4},... | collective-permute-start | bytes 1179656 | tf_op jit(solution)/shard_map/cond/branch_1_fun/ppermute | solution.py:357
  46.7 30.3 %collective-permute-start.39 = (bf16[8,2,32,384]{3,2,1,0:T(8,128)(2,1)}, bf16[8,2,32,384]{3,2,1,0:T(8,128)(2,1)}, u32[]{:S(2)}, u32[]{:S(2)}) collective-permute-start(bf16[8,2,32,384]{3,2,1,0:T(8,128)(2,1)} %get-tuple-element.187), channel_id=1, source_target_pairs={{0,2},{1,3},{4,6},{5,7},{8,10},{9,11},{12,14},{13,15},{16,18},{17,... | collective-permute-start | bytes 1179656 | tf_op jit(solution)/shard_map/cond/branch_1_fun/ppermute | solution.py:351
  64.6 48.5 %collective-permute-start.38 = (bf16[8,2,32,384]{3,2,1,0:T(8,128)(2,1)}, bf16[8,2,32,384]{3,2,1,0:T(8,128)(2,1)}, u32[]{:S(2)}, u32[]{:S(2)}) collective-permute-start(bf16[8,2,32,384]{3,2,1,0:T(8,128)(2,1)} %get-tuple-element.187), channel_id=1, source_target_pairs={{2,12},{6,8},{10,4},{14,0},{18,28},{22,24},{26,20},{30,16}} | collective-permute-start | bytes 1179656 | tf_op jit(solution)/shard_map/cond/branch_1_fun/ppermute | solution.py:357
  73.1 38.8 %collective-permute-start.37 = (bf16[8,2,32,384]{3,2,1,0:T(8,128)(2,1)}, bf16[8,2,32,384]{3,2,1,0:T(8,128)(2,1)}, u32[]{:S(2)}, u32[]{:S(2)}) collective-permute-start(bf16[8,2,32,384]{3,2,1,0:T(8,128)(2,1)} %get-tuple-element.186), channel_id=1, source_target_pairs={{0,6},{1,7},{2,4},{3,5},{4,2},{5,3},{6,0},{7,1},{16,22},{17,23},{1... | collective-permute-start | bytes 1179656 | tf_op jit(solution)/shard_map/cond/branch_1_fun/ppermute | solution.py:357
  75.0 40.1 %collective-permute-start.41 = (bf16[8,2,32,384]{3,2,1,0:T(8,128)(2,1)}, bf16[8,2,32,384]{3,2,1,0:T(8,128)(2,1)}, u32[]{:S(2)}, u32[]{:S(2)}) collective-permute-start(bf16[8,2,32,384]{3,2,1,0:T(8,128)(2,1)} %get-tuple-element.188), channel_id=1, source_target_pairs={{0,11},{1,10},{2,9},{3,8},{8,3},{9,2},{10,1},{11,0},{16,27},{17,26... | collective-permute-start | bytes 1179656 | tf_op jit(solution)/shard_map/cond/branch_1_fun/ppermute | solution.py:357
  76.9 42.4 %collective-permute-start.40 = (bf16[8,2,32,384]{3,2,1,0:T(8,128)(2,1)}, bf16[8,2,32,384]{3,2,1,0:T(8,128)(2,1)}, u32[]{:S(2)}, u32[]{:S(2)}) collective-permute-start(bf16[8,2,32,384]{3,2,1,0:T(8,128)(2,1)} %collective-permute-done.39), channel_id=1, source_target_pairs={{2,14},{3,15},{6,10},{7,11},{10,6},{11,7},{14,2},{15,3},{18,30},{1... | collective-permute-start | bytes 1179656 | tf_op jit(solution)/shard_map/cond/branch_1_fun/ppermute | solution.py:352
  86.4 38.0 %collective-permute-start.42 = (bf16[8,2,32,384]{3,2,1,0:T(8,128)(2,1)}, bf16[8,2,32,384]{3,2,1,0:T(8,128)(2,1)S(1)}, u32[]{:S(2)}, u32[]{:S(2)}) collective-permute-start(bf16[8,2,32,384]{3,2,1,0:T(8,128)(2,1)} %get-tuple-element.189), channel_id=1, source_target_pairs={{0,7},{1,6},{2,5},{3,4},{4,3},{5,2},{6,1},{7,0},{16,23},{17,22},{1... | collective-permute-start | bytes 1179656 | tf_op jit(solution)/shard_map/cond/branch_1_fun/ppermute | solution.py:357
  162.0 26.5 %collective-permute-start.47 = (bf16[8,2,32,384]{3,2,1,0:T(8,128)(2,1)}, bf16[8,2,32,384]{3,2,1,0:T(8,128)(2,1)S(1)}, u32[]{:S(2)}, u32[]{:S(2)}) collective-permute-start(bf16[8,2,32,384]{3,2,1,0:T(8,128)(2,1)} %get-tuple-element.197), channel_id=1, source_target_pairs={{0,8},{1,9},{2,10},{3,11},{4,12},{8,0},{9,1},{10,2},{11,3},{12,4},... | collective-permute-start | bytes 1179656 | tf_op jit(solution)/shard_map/cond/branch_1_fun/ppermute | solution.py:357
  163.9 29.1 %collective-permute-start.48 = (bf16[8,2,32,384]{3,2,1,0:T(8,128)(2,1)}, bf16[8,2,32,384]{3,2,1,0:T(8,128)(2,1)S(1)}, u32[]{:S(2)}, u32[]{:S(2)}) collective-permute-start(bf16[8,2,32,384]{3,2,1,0:T(8,128)(2,1)} %get-tuple-element.198), channel_id=1, source_target_pairs={{0,4},{1,5},{2,6},{3,7},{4,0},{5,1},{6,2},{7,3},{16,20},{17,21},{1... | collective-permute-start | bytes 1179656 | tf_op jit(solution)/shard_map/cond/branch_1_fun/ppermute | solution.py:357
  165.8 29.1 %collective-permute-start.49 = (bf16[8,2,32,384]{3,2,1,0:T(8,128)(2,1)}, bf16[8,2,32,384]{3,2,1,0:T(8,128)(2,1)S(1)}, u32[]{:S(2)}, u32[]{:S(2)}) collective-permute-start(bf16[8,2,32,384]{3,2,1,0:T(8,128)(2,1)} %get-tuple-element.199), channel_id=1, source_target_pairs={{0,12},{1,13},{2,14},{4,8},{5,9},{6,10},{8,4},{9,5},{10,6},{12,0},... | collective-permute-start | bytes 1179656 | tf_op jit(solution)/shard_map/cond/branch_1_fun/ppermute | solution.py:357
  167.8 46.2 %collective-permute-start.50 = (bf16[8,2,32,384]{3,2,1,0:T(8,128)(2,1)}, bf16[8,2,32,384]{3,2,1,0:T(8,128)(2,1)S(1)}, u32[]{:S(2)}, u32[]{:S(2)}) collective-permute-start(bf16[8,2,32,384]{3,2,1,0:T(8,128)(2,1)} %get-tuple-element.200), channel_id=1, source_target_pairs={{0,9},{1,8},{2,11},{3,10},{8,1},{9,0},{10,3},{11,2},{16,25},{17,24... | collective-permute-start | bytes 1179656 | tf_op jit(solution)/shard_map/cond/branch_1_fun/ppermute | solution.py:357
  173.1 51.2 %collective-permute-start.51 = (bf16[8,2,32,384]{3,2,1,0:T(8,128)(2,1)}, bf16[8,2,32,384]{3,2,1,0:T(8,128)(2,1)S(1)}, u32[]{:S(2)}, u32[]{:S(2)}) collective-permute-start(bf16[8,2,32,384]{3,2,1,0:T(8,128)(2,1)} %get-tuple-element.201), channel_id=1, source_target_pairs={{0,5},{1,4},{2,7},{3,6},{4,1},{5,0},{6,3},{7,2},{16,21},{17,20},{1... | collective-permute-start | bytes 1179656 | tf_op jit(solution)/shard_map/cond/branch_1_fun/ppermute | solution.py:357
  188.5 50.8 %collective-permute-start.52 = (bf16[8,2,32,384]{3,2,1,0:T(8,128)(2,1)}, bf16[8,2,32,384]{3,2,1,0:T(8,128)(2,1)S(1)}, u32[]{:S(2)}, u32[]{:S(2)}) collective-permute-start(bf16[8,2,32,384]{3,2,1,0:T(8,128)(2,1)} %get-tuple-element.202), channel_id=1, source_target_pairs={{0,13},{1,12},{2,15},{3,14},{4,9},{5,8},{6,11},{7,10},{8,5},{9,4},... | collective-permute-start | bytes 1179656 | tf_op jit(solution)/shard_map/cond/branch_1_fun/ppermute | solution.py:357
  193.0 50.8 %collective-permute-start.53 = (bf16[8,2,32,384]{3,2,1,0:T(8,128)(2,1)}, bf16[8,2,32,384]{3,2,1,0:T(8,128)(2,1)S(1)}, u32[]{:S(2)}, u32[]{:S(2)}) collective-permute-start(bf16[8,2,32,384]{3,2,1,0:T(8,128)(2,1)} %get-tuple-element.203), channel_id=1, source_target_pairs={{0,10},{1,11},{2,8},{3,9},{8,2},{9,3},{10,0},{11,1},{16,26},{17,27... | collective-permute-start | bytes 1179656 | tf_op jit(solution)/shard_map/cond/branch_1_fun/ppermute | solution.py:357
  195.0 54.1 %collective-permute-start.54 = (bf16[8,2,32,384]{3,2,1,0:T(8,128)(2,1)}, bf16[8,2,32,384]{3,2,1,0:T(8,128)(2,1)}, u32[]{:S(2)}, u32[]{:S(2)}) collective-permute-start(bf16[8,2,32,384]{3,2,1,0:T(8,128)(2,1)} %get-tuple-element.204), channel_id=1, source_target_pairs={{0,6},{1,7},{2,4},{3,5},{4,2},{5,3},{6,0},{7,1},{16,22},{17,23},{1... | collective-permute-start | bytes 1179656 | tf_op jit(solution)/shard_map/cond/branch_1_fun/ppermute | solution.py:357
  214.0 45.4 %collective-permute-start.55 = (bf16[8,2,32,384]{3,2,1,0:T(8,128)(2,1)}, bf16[8,2,32,384]{3,2,1,0:T(8,128)(2,1)}, u32[]{:S(2)}, u32[]{:S(2)}) collective-permute-start(bf16[8,2,32,384]{3,2,1,0:T(8,128)(2,1)} %get-tuple-element.205), channel_id=1, source_target_pairs={{0,14},{2,12},{3,13},{4,10},{6,8},{7,9},{8,6},{10,4},{11,5},{12,2}... | collective-permute-start | bytes 1179656 | tf_op jit(solution)/shard_map/cond/branch_1_fun/ppermute | solution.py:357
  224.3 37.0 %collective-permute-start.56 = (bf16[8,2,32,384]{3,2,1,0:T(8,128)(2,1)}, bf16[8,2,32,384]{3,2,1,0:T(8,128)(2,1)}, u32[]{:S(2)}, u32[]{:S(2)}) collective-permute-start(bf16[8,2,32,384]{3,2,1,0:T(8,128)(2,1)} %get-tuple-element.206), channel_id=1, source_target_pairs={{0,11},{1,10},{2,9},{3,8},{8,3},{9,2},{10,1},{11,0},{16,27},{17,26... | collective-permute-start | bytes 1179656 | tf_op jit(solution)/shard_map/cond/branch_1_fun/ppermute | solution.py:357
  228.0 36.5 %all-to-all-start.1 = ((f32[16,24,128]{2,1,0:T(8,128)}), f32[16,24,128]{2,1,0:T(8,128)S(1)}, u32[]{:S(2)}, u32[]{:S(2)}) async-start(f32[16,24,128]{2,1,0:T(8,128)} %broadcast_in_dim.15), calls=%async_computation.1 | async-start | bytes 393216 | tf_op jit(solution)/shard_map/cond/branch_1_fun/all_to_all | solution.py:412
  239.3 27.6 %collective-permute-start.57 = (bf16[8,2,32,384]{3,2,1,0:T(8,128)(2,1)}, bf16[8,2,32,384]{3,2,1,0:T(8,128)(2,1)}, u32[]{:S(2)}, u32[]{:S(2)}) collective-permute-start(bf16[8,2,32,384]{3,2,1,0:T(8,128)(2,1)} %get-tuple-element.207), channel_id=1, source_target_pairs={{0,7},{1,6},{2,5},{3,4},{4,3},{5,2},{6,1},{7,0},{16,23},{17,22},{1... | collective-permute-start | bytes 1179656 | tf_op jit(solution)/shard_map/cond/branch_1_fun/ppermute | solution.py:357
  249.0 26.4 %collective-permute-start.59 = (bf16[8,2,32,384]{3,2,1,0:T(8,128)(2,1)}, bf16[8,2,32,384]{3,2,1,0:T(8,128)(2,1)}, u32[]{:S(2)}, u32[]{:S(2)}) collective-permute-start(bf16[8,2,32,384]{3,2,1,0:T(8,128)(2,1)} %get-tuple-element.209), channel_id=1, source_target_pairs={{0,3},{1,2},{2,1},{3,0},{4,7},{5,6},{6,5},{7,4},{16,19},{17,18},{1... | collective-permute-start | bytes 1179656 | tf_op jit(solution)/shard_map/cond/branch_1_fun/ppermute | solution.py:357
  (37 other events, 1624.4 us)

commit v2 on v1

--- a/solution.py
+++ b/solution.py
@@ -45,7 +45,8 @@
     order = [0]
     for t in range(quarter):
         order += [2 * quarter + t, quarter + t, 3 * quarter + t]
-    return order + list(range(quarter - 1, 0, -1))
+        order += [quarter - 1 - t] if t < quarter - 1 else []
+    return order
 
 
 def forward_kernel(devices, group, waves, pos_ref, spec_ref, basis_ref, trunc_ref, perm_ref, *rest):
@@ -341,10 +342,13 @@
     return cos.reshape(size, size).astype(BF16), (-sin).reshape(size, size).astype(BF16)
 
 
+def relay_shifts(devices):
+    hop = devices // 8
+    return hop, devices // 4 * 3 + hop
+
+
 def exchange(arrays, devices, needed, relay=False):
-    quarter = devices // 4
-    hop = quarter // 2
-    far = 3 * quarter + hop
+    hop, far = relay_shifts(devices)
     handed = [d for d in range(devices) if relay and hop and not d & hop and needed(d, d ^ far)]
     order = exchange_order(devices)
     if handed:
@@ -370,9 +374,8 @@
     pos = position.reshape(1)
     spec = jnp.swapaxes(spectral, 2, 3)
     order = latitude_order(half_lats, devices)
-    lats = jnp.arange(half_lats, dtype=jnp.int32)
-    perm = (lats[:, None] == order[None, :]).astype(BF16)
-    back = (order[:, None] == lats[None, :]).astype(BF16)
+    perm = np.eye(half_lats, dtype=BF16)[:, order]
+    perm, back = jnp.array(perm), jnp.array(np.ascontiguousarray(perm.T))
     trunc_row = trunc.reshape(1, half_lats)
     weight_row = quad_weights.reshape(1, half_lats)
     blocks = forward(pos, spec, basis, trunc_row, perm, devices)
@@ -391,7 +394,7 @@
         total = devices * waves
         cosine, sine = fourier_tables(total)
         sign = 1 - 2 * (jnp.arange(total, dtype=jnp.int32) % 2)
-        middle = jnp.broadcast_to(sign.astype(BF16), (8, total))
+        middle = jnp.array(np.tile(1 - 2 * (np.arange(total) % 2), (8, 1)).astype(BF16))
         mix = jnp.kron(jnp.eye(4, dtype=F32), column.T).astype(BF16)
         coef = jnp.stack([jnp.tile(square_coef, 4), jnp.tile(cube_coef, 4)])
         sums = 2.0 * jnp.sum(cosine.astype(F32), axis=1) - cosine[:, 0].astype(F32)

time: 301 us -> 298 us (0.990)
  the two profiles are of different devices: /device:TPU:1 before, /device:TPU:9 now
where the time goes in v2:
time: 298 us; the launch traced here: 297 us
  starting transfers between devices  172 us (58%)
  waiting for transfers between devices  52.7 us (18%)
  Pallas kernels  45.6 us (15%)
  local copies, waits for them, and re-layouts  12.2 us (4%)
  other arithmetic  11.2 us (4%)
    ppermute x30, starting transfers between devices, exchange(): array = lax.ppermute(array, 'wave', pairs)  148 us
    ppermute x30, waiting for transfers between devices, exchange(): array = lax.ppermute(array, 'wave', pairs)  52.7 us
    pallas_call x1, Pallas kernels, on_grid(): pl.pallas_call(functools.partial(grid_kernel, devices, waves, unroll), gr...  19.1 us
    all_to_all x1, starting transfers between devices, finish(): lax.all_to_all(sent, 'wave', split_axis=0, concat_axis=0, tiled=True)  16.1 us
    pallas_call x1, Pallas kernels, inverse(): pl.pallas_call(functools.partial(inverse_kernel, devices, group, waves, u...  14.8 us
    pallas_call x1, Pallas kernels, forward(): pl.pallas_call(functools.partial(forward_kernel, devices, group, waves),...  11.7 us
    ppermute x1, starting transfers between devices, exchange(): lax.ppermute(arrays[order.index(far)], 'wave', [(d, d ^ hop) for d in han...  7.08 us
  transfers between devices with their start and end apart: 33, of which 8 were waited for; matrix products, arithmetic and copies ran while one was open for 7% of the time, Pallas kernels for 0%

profile of v2, /device:TPU:9, one launch (start us, length us, event | category | flops | bytes accessed | tf_op | source)
XLA Modules:
  0.0 296.5 jit_solution(12596420980179218163)
XLA Ops:
  2.1 11.7 %forward.1 = (bf16[8,2,32,384]{3,2,1,0:T(8,128)(2,1)S(1)}, bf16[8,2,32,384]{3,2,1,0:T(8,128)(2,1)}, bf16[8,2,32,384]{3,2,1,0:T(8,128)(2,1)}, bf16[8,2,32,384]{3,...) custom-call(s32[1]{0:T(128)} %bitcast.12.pos_ref, ...), custom_call_target="tpu_custom_call" | custom-call | tf_op jit(solution)/shard_map/forward/pallas_call | solution.py:102
  13.8 282.5 %conditional.1 = (bf16[32,2,192,256]{3,2,1,0:T(8,128)(2,1)}) conditional(s32[]{:T(128)} %convert_element_type.121, (s32[]{:T(128)}, f32[96,96]{1,0:T(8,128)S(1)}, f32[96]{0:T(128)}, f32[96]{0:T(128)}, bf16[8,2,32,384]{3,2,1,0:T(8,128)(2,1)}, /*index=5*/bf16[8,2,32,384]{3,2,1,0:T(8,128)(2,1)}, bf16[8,2,32,384]{3,2,1,0:T(8,128)(2,1)}, ...), branch_computations={%region_1.5_spmd, %region_5.9_spmd} | conditional | flops 3923156 | bytes 84554960 | solution.py:430
  14.5 5.6 %collective-permute-start.31 = (bf16[8,2,32,384]{3,2,1,0:T(8,128)(2,1)}, bf16[8,2,32,384]{3,2,1,0:T(8,128)(2,1)S(1)}, u32[]{:S(2)}, u32[]{:S(2)}) collective-permute-start(bf16[8,2,32,384]{3,2,1,0:T(8,128)(2,1)} %get-tuple-element.186), channel_id=1, source_target_pairs={{0,4},{1,5},{2,6},{3,7},{4,0},{5,1},{6,2},{7,3},{16,20},{17,21},{1... | collective-permute-start | bytes 1179656 | tf_op jit(solution)/shard_map/cond/branch_1_fun/ppermute | solution.py:361
  22.1 4.3 %collective-permute-start.33 = (bf16[8,2,32,384]{3,2,1,0:T(8,128)(2,1)}, bf16[8,2,32,384]{3,2,1,0:T(8,128)(2,1)S(1)}, u32[]{:S(2)}, u32[]{:S(2)}) collective-permute-start(bf16[8,2,32,384]{3,2,1,0:T(8,128)(2,1)} %get-tuple-element.188), channel_id=1, source_target_pairs={{0,3},{1,2},{2,1},{3,0},{4,7},{5,6},{6,5},{7,4},{16,19},{17,18},{1... | collective-permute-start | bytes 1179656 | tf_op jit(solution)/shard_map/cond/branch_1_fun/ppermute | solution.py:361
  30.0 13.8 %collective-permute-start.35 = (bf16[8,2,32,384]{3,2,1,0:T(8,128)(2,1)}, bf16[8,2,32,384]{3,2,1,0:T(8,128)(2,1)S(1)}, u32[]{:S(2)}, u32[]{:S(2)}) collective-permute-start(bf16[8,2,32,384]{3,2,1,0:T(8,128)(2,1)} %get-tuple-element.190), channel_id=1, source_target_pairs={{0,5},{1,4},{2,7},{3,6},{4,1},{5,0},{6,3},{7,2},{16,21},{17,20},{1... | collective-permute-start | bytes 1179656 | tf_op jit(solution)/shard_map/cond/branch_1_fun/ppermute | solution.py:361
  43.9 7.1 %collective-permute-start.41 = (bf16[8,2,32,384]{3,2,1,0:T(8,128)(2,1)}, bf16[8,2,32,384]{3,2,1,0:T(8,128)(2,1)}, u32[]{:S(2)}, u32[]{:S(2)}) collective-permute-start(bf16[8,2,32,384]{3,2,1,0:T(8,128)(2,1)} %get-tuple-element.195), channel_id=1, source_target_pairs={{0,2},{1,3},{4,6},{5,7},{8,10},{9,11},{12,14},{13,15},{16,18},{17,... | collective-permute-start | bytes 1179656 | tf_op jit(solution)/shard_map/cond/branch_1_fun/ppermute | solution.py:355
  54.2 6.2 %collective-permute-start.36 = (bf16[8,2,32,384]{3,2,1,0:T(8,128)(2,1)}, bf16[8,2,32,384]{3,2,1,0:T(8,128)(2,1)}, u32[]{:S(2)}, u32[]{:S(2)}) collective-permute-start(bf16[8,2,32,384]{3,2,1,0:T(8,128)(2,1)} %get-tuple-element.191), channel_id=1, source_target_pairs={{0,13},{1,12},{2,15},{3,14},{4,9},{5,8},{6,11},{7,10},{8,5},{9,4},... | collective-permute-start | bytes 1179656 | tf_op jit(solution)/shard_map/cond/branch_1_fun/ppermute | solution.py:361
  60.4 4.2 %collective-permute-start.37 = (bf16[8,2,32,384]{3,2,1,0:T(8,128)(2,1)}, bf16[8,2,32,384]{3,2,1,0:T(8,128)(2,1)}, u32[]{:S(2)}, u32[]{:S(2)}) collective-permute-start(bf16[8,2,32,384]{3,2,1,0:T(8,128)(2,1)} %get-tuple-element.192), channel_id=1, source_target_pairs={{0,2},{1,3},{2,0},{3,1},{4,6},{5,7},{6,4},{7,5},{16,18},{17,19},{1... | collective-permute-start | bytes 1179656 | tf_op jit(solution)/shard_map/cond/branch_1_fun/ppermute | solution.py:361
  64.6 4.6 %collective-permute-done.35.rest_6_ = bf16[8,2,32,384]{3,2,1,0:T(8,128)(2,1)S(1)} collective-permute-done((bf16[8,2,32,384]{3,2,1,0:T(8,128)(2,1)}, bf16[8,2,32,384]{3,2,1,0:T(8,128)(2,1)S(1)}, u32[]{:S(2)}, u32[]{:S(2)}) %collective-permute-start.35) | collective-permute-done | bytes 393248 | tf_op jit(solution)/shard_map/cond/branch_1_fun/ppermute | solution.py:361
  79.7 5.0 %collective-permute-done.36.rest_7_ = bf16[8,2,32,384]{3,2,1,0:T(8,128)(2,1)} collective-permute-done((bf16[8,2,32,384]{3,2,1,0:T(8,128)(2,1)}, bf16[8,2,32,384]{3,2,1,0:T(8,128)(2,1)}, u32[]{:S(2)}, u32[]{:S(2)}) %collective-permute-start.36) | collective-permute-done | bytes 393248 | tf_op jit(solution)/shard_map/cond/branch_1_fun/ppermute | solution.py:361
  89.3 5.9 %collective-permute-start.45 = (bf16[8,2,32,384]{3,2,1,0:T(8,128)(2,1)}, bf16[8,2,32,384]{3,2,1,0:T(8,128)(2,1)S(1)}, u32[]{:S(2)}, u32[]{:S(2)}) collective-permute-start(bf16[8,2,32,384]{3,2,1,0:T(8,128)(2,1)} %get-tuple-element.198), channel_id=1, source_target_pairs={{0,7},{1,6},{2,5},{3,4},{4,3},{5,2},{6,1},{7,0},{16,23},{17,22},{1... | collective-permute-start | bytes 1179656 | tf_op jit(solution)/shard_map/cond/branch_1_fun/ppermute | solution.py:361
  95.2 30.1 %collective-permute-start.46 = (bf16[8,2,32,384]{3,2,1,0:T(8,128)(2,1)}, bf16[8,2,32,384]{3,2,1,0:T(8,128)(2,1)S(1)}, u32[]{:S(2)}, u32[]{:S(2)}) collective-permute-start(bf16[8,2,32,384]{3,2,1,0:T(8,128)(2,1)} %get-tuple-element.199), channel_id=1, source_target_pairs={{0,15},{1,14},{3,12},{4,11},{5,10},{7,8},{8,7},{9,6},{11,4},{12,3}... | collective-permute-start | bytes 1179656 | tf_op jit(solution)/shard_map/cond/branch_1_fun/ppermute | solution.py:361
  128.6 9.7 %collective-permute-done.46.rest_15_ = bf16[8,2,32,384]{3,2,1,0:T(8,128)(2,1)S(1)} collective-permute-done((bf16[8,2,32,384]{3,2,1,0:T(8,128)(2,1)}, bf16[8,2,32,384]{3,2,1,0:T(8,128)(2,1)S(1)}, u32[]{:S(2)}, u32[]{:S(2)}) %collective-permute-start.46) | collective-permute-done | bytes 393248 | tf_op jit(solution)/shard_map/cond/branch_1_fun/ppermute | solution.py:361
  139.0 19.1 %grid.3 = (bf16[8,2,32,384]{3,2,1,0:T(8,128)(2,1)}, bf16[8,2,32,384]{3,2,1,0:T(8,128)(2,1)}, bf16[8,2,32,384]{3,2,1,0:T(8,128)(2,1)}, bf16[8,2,32,384]{3,2,1,0:T...) custom-call(s32[1]{0:T(128)} %get-tuple-element.169.pos_ref, ...), custom_call_target="tpu_custom_call" | custom-call | tf_op jit(solution)/shard_map/cond/branch_1_fun/grid/pallas_call | solution.py:207
  158.8 17.2 %collective-permute-start.48 = (bf16[8,2,32,384]{3,2,1,0:T(8,128)(2,1)}, bf16[8,2,32,384]{3,2,1,0:T(8,128)(2,1)S(1)}, u32[]{:S(2)}, u32[]{:S(2)}) collective-permute-start(bf16[8,2,32,384]{3,2,1,0:T(8,128)(2,1)} %get-tuple-element.204), channel_id=1, source_target_pairs={{0,4},{1,5},{2,6},{3,7},{4,0},{5,1},{6,2},{7,3},{16,20},{17,21},{1... | collective-permute-start | bytes 1179656 | tf_op jit(solution)/shard_map/cond/branch_1_fun/ppermute | solution.py:361
  181.9 16.5 %collective-permute-start.52 = (bf16[8,2,32,384]{3,2,1,0:T(8,128)(2,1)}, bf16[8,2,32,384]{3,2,1,0:T(8,128)(2,1)S(1)}, u32[]{:S(2)}, u32[]{:S(2)}) collective-permute-start(bf16[8,2,32,384]{3,2,1,0:T(8,128)(2,1)} %get-tuple-element.208), channel_id=1, source_target_pairs={{0,5},{1,4},{2,7},{3,6},{4,1},{5,0},{6,3},{7,2},{16,21},{17,20},{1... | collective-permute-start | bytes 1179656 | tf_op jit(solution)/shard_map/cond/branch_1_fun/ppermute | solution.py:361
  205.2 6.2 %collective-permute-start.56 = (bf16[8,2,32,384]{3,2,1,0:T(8,128)(2,1)}, bf16[8,2,32,384]{3,2,1,0:T(8,128)(2,1)}, u32[]{:S(2)}, u32[]{:S(2)}) collective-permute-start(bf16[8,2,32,384]{3,2,1,0:T(8,128)(2,1)} %get-tuple-element.212), channel_id=1, source_target_pairs={{0,6},{1,7},{2,4},{3,5},{4,2},{5,3},{6,0},{7,1},{16,22},{17,23},{1... | collective-permute-start | bytes 1179656 | tf_op jit(solution)/shard_map/cond/branch_1_fun/ppermute | solution.py:361
  213.1 16.1 %all-to-all-start.1 = ((f32[16,24,128]{2,1,0:T(8,128)}), f32[16,24,128]{2,1,0:T(8,128)S(1)}, u32[]{:S(2)}, u32[]{:S(2)}) async-start(f32[16,24,128]{2,1,0:T(8,128)} %broadcast_in_dim.11), calls=%async_computation.1 | async-start | bytes 393216 | tf_op jit(solution)/shard_map/cond/branch_1_fun/all_to_all | solution.py:415
  231.7 5.3 %collective-permute-start.58 = (bf16[8,2,32,384]{3,2,1,0:T(8,128)(2,1)}, bf16[8,2,32,384]{3,2,1,0:T(8,128)(2,1)}, u32[]{:S(2)}, u32[]{:S(2)}) collective-permute-start(bf16[8,2,32,384]{3,2,1,0:T(8,128)(2,1)} %get-tuple-element.214), channel_id=1, source_target_pairs={{0,1},{1,0},{2,3},{3,2},{4,5},{5,4},{6,7},{7,6},{16,17},{17,16},{1... | collective-permute-start | bytes 1179656 | tf_op jit(solution)/shard_map/cond/branch_1_fun/ppermute | solution.py:361
  238.4 9.3 %collective-permute-start.60 = (bf16[8,2,32,384]{3,2,1,0:T(8,128)(2,1)}, bf16[8,2,32,384]{3,2,1,0:T(8,128)(2,1)}, u32[]{:S(2)}, u32[]{:S(2)}) collective-permute-start(bf16[8,2,32,384]{3,2,1,0:T(8,128)(2,1)} %get-tuple-element.216), channel_id=1, source_target_pairs={{0,7},{1,6},{2,5},{3,4},{4,3},{5,2},{6,1},{7,0},{16,23},{17,22},{1... | collective-permute-start | bytes 1179656 | tf_op jit(solution)/shard_map/cond/branch_1_fun/ppermute | solution.py:361
  247.7 10.3 %collective-permute-done.56.rest_10_ = bf16[8,2,32,384]{3,2,1,0:T(8,128)(2,1)} collective-permute-done((bf16[8,2,32,384]{3,2,1,0:T(8,128)(2,1)}, bf16[8,2,32,384]{3,2,1,0:T(8,128)(2,1)}, u32[]{:S(2)}, u32[]{:S(2)}) %collective-permute-start.56) | collective-permute-done | bytes 393248 | tf_op jit(solution)/shard_map/cond/branch_1_fun/ppermute | solution.py:361
  265.0 6.6 %collective-permute-done.60.rest_14_ = bf16[8,2,32,384]{3,2,1,0:T(8,128)(2,1)} collective-permute-done((bf16[8,2,32,384]{3,2,1,0:T(8,128)(2,1)}, bf16[8,2,32,384]{3,2,1,0:T(8,128)(2,1)}, u32[]{:S(2)}, u32[]{:S(2)}) %collective-permute-start.60) | collective-permute-done | bytes 393248 | tf_op jit(solution)/shard_map/cond/branch_1_fun/ppermute | solution.py:361
  271.6 9.7 %collective-permute-done.61.rest_15_ = bf16[8,2,32,384]{3,2,1,0:T(8,128)(2,1)} collective-permute-done((bf16[8,2,32,384]{3,2,1,0:T(8,128)(2,1)}, bf16[8,2,32,384]{3,2,1,0:T(8,128)(2,1)}, u32[]{:S(2)}, u32[]{:S(2)}) %collective-permute-start.61) | collective-permute-done | bytes 393248 | tf_op jit(solution)/shard_map/cond/branch_1_fun/ppermute | solution.py:361
  281.3 14.8 %inverse.3 = bf16[32,2,192,256]{3,2,1,0:T(8,128)(2,1)} custom-call(s32[1]{0:T(128)} %get-tuple-element.169.pos_ref, f32[64]{0:T(128)} %reshape.550.sums_ref, bf16[32,2,192,256]{3,2,1,0:T(8,128)(2,1)} %get-tuple-element.175.spec_ref, bf16[32,2,256,256]{3,2,1,0:T(8,128)(2,1)} %get-tuple-element.176.basis_ref, s32[1,256]{1,0:T(1,128)S(1)} %get-tuple-element.177.trunc_ref, ...), custom_call_target="tpu_custom_call" | custom-call | tf_op jit(solution)/shard_map/cond/branch_1_fun/inverse/pallas_call | solution.py:303
  (165 shorter events, 54.9 us)
Async XLA Ops:
  14.5 29.3 %collective-permute-start.31 = (bf16[8,2,32,384]{3,2,1,0:T(8,128)(2,1)}, bf16[8,2,32,384]{3,2,1,0:T(8,128)(2,1)S(1)}, u32[]{:S(2)}, u32[]{:S(2)}) collective-permute-start(bf16[8,2,32,384]{3,2,1,0:T(8,128)(2,1)} %get-tuple-element.186), channel_id=1, source_target_pairs={{0,4},{1,5},{2,6},{3,7},{4,0},{5,1},{6,2},{7,3},{16,20},{17,21},{1... | collective-permute-start | bytes 1179656 | tf_op jit(solution)/shard_map/cond/branch_1_fun/ppermute | solution.py:361
  20.2 32.6 %collective-permute-start.32 = (bf16[8,2,32,384]{3,2,1,0:T(8,128)(2,1)}, bf16[8,2,32,384]{3,2,1,0:T(8,128)(2,1)S(1)}, u32[]{:S(2)}, u32[]{:S(2)}) collective-permute-start(bf16[8,2,32,384]{3,2,1,0:T(8,128)(2,1)} %get-tuple-element.187), channel_id=1, source_target_pairs={{0,12},{1,13},{2,14},{4,8},{5,9},{6,10},{8,4},{9,5},{10,6},{12,0},... | collective-permute-start | bytes 1179656 | tf_op jit(solution)/shard_map/cond/branch_1_fun/ppermute | solution.py:361
  22.1 32.1 %collective-permute-start.33 = (bf16[8,2,32,384]{3,2,1,0:T(8,128)(2,1)}, bf16[8,2,32,384]{3,2,1,0:T(8,128)(2,1)S(1)}, u32[]{:S(2)}, u32[]{:S(2)}) collective-permute-start(bf16[8,2,32,384]{3,2,1,0:T(8,128)(2,1)} %get-tuple-element.188), channel_id=1, source_target_pairs={{0,3},{1,2},{2,1},{3,0},{4,7},{5,6},{6,5},{7,4},{16,19},{17,18},{1... | collective-permute-start | bytes 1179656 | tf_op jit(solution)/shard_map/cond/branch_1_fun/ppermute | solution.py:361
  26.4 34.1 %collective-permute-start.34 = (bf16[8,2,32,384]{3,2,1,0:T(8,128)(2,1)}, bf16[8,2,32,384]{3,2,1,0:T(8,128)(2,1)S(1)}, u32[]{:S(2)}, u32[]{:S(2)}) collective-permute-start(bf16[8,2,32,384]{3,2,1,0:T(8,128)(2,1)} %get-tuple-element.189), channel_id=1, source_target_pairs={{0,9},{1,8},{2,11},{3,10},{8,1},{9,0},{10,3},{11,2},{16,25},{17,24... | collective-permute-start | bytes 1179656 | tf_op jit(solution)/shard_map/cond/branch_1_fun/ppermute | solution.py:361
  30.0 39.2 %collective-permute-start.35 = (bf16[8,2,32,384]{3,2,1,0:T(8,128)(2,1)}, bf16[8,2,32,384]{3,2,1,0:T(8,128)(2,1)S(1)}, u32[]{:S(2)}, u32[]{:S(2)}) collective-permute-start(bf16[8,2,32,384]{3,2,1,0:T(8,128)(2,1)} %get-tuple-element.190), channel_id=1, source_target_pairs={{0,5},{1,4},{2,7},{3,6},{4,1},{5,0},{6,3},{7,2},{16,21},{17,20},{1... | collective-permute-start | bytes 1179656 | tf_op jit(solution)/shard_map/cond/branch_1_fun/ppermute | solution.py:361
  43.9 26.8 %collective-permute-start.41 = (bf16[8,2,32,384]{3,2,1,0:T(8,128)(2,1)}, bf16[8,2,32,384]{3,2,1,0:T(8,128)(2,1)}, u32[]{:S(2)}, u32[]{:S(2)}) collective-permute-start(bf16[8,2,32,384]{3,2,1,0:T(8,128)(2,1)} %get-tuple-element.195), channel_id=1, source_target_pairs={{0,2},{1,3},{4,6},{5,7},{8,10},{9,11},{12,14},{13,15},{16,18},{17,... | collective-permute-start | bytes 1179656 | tf_op jit(solution)/shard_map/cond/branch_1_fun/ppermute | solution.py:355
  52.8 36.5 %collective-permute-start.40 = (bf16[8,2,32,384]{3,2,1,0:T(8,128)(2,1)}, bf16[8,2,32,384]{3,2,1,0:T(8,128)(2,1)}, u32[]{:S(2)}, u32[]{:S(2)}) collective-permute-start(bf16[8,2,32,384]{3,2,1,0:T(8,128)(2,1)} %get-tuple-element.195), channel_id=1, source_target_pairs={{2,12},{6,8},{10,4},{14,0},{18,28},{22,24},{26,20},{30,16}} | collective-permute-start | bytes 1179656 | tf_op jit(solution)/shard_map/cond/branch_1_fun/ppermute | solution.py:361
  54.2 30.5 %collective-permute-start.36 = (bf16[8,2,32,384]{3,2,1,0:T(8,128)(2,1)}, bf16[8,2,32,384]{3,2,1,0:T(8,128)(2,1)}, u32[]{:S(2)}, u32[]{:S(2)}) collective-permute-start(bf16[8,2,32,384]{3,2,1,0:T(8,128)(2,1)} %get-tuple-element.191), channel_id=1, source_target_pairs={{0,13},{1,12},{2,15},{3,14},{4,9},{5,8},{6,11},{7,10},{8,5},{9,4},... | collective-permute-start | bytes 1179656 | tf_op jit(solution)/shard_map/cond/branch_1_fun/ppermute | solution.py:361
  84.7 43.8 %collective-permute-start.39 = (bf16[8,2,32,384]{3,2,1,0:T(8,128)(2,1)}, bf16[8,2,32,384]{3,2,1,0:T(8,128)(2,1)S(1)}, u32[]{:S(2)}, u32[]{:S(2)}) collective-permute-start(bf16[8,2,32,384]{3,2,1,0:T(8,128)(2,1)} %get-tuple-element.194), channel_id=1, source_target_pairs={{0,6},{1,7},{2,4},{3,5},{4,2},{5,3},{6,0},{7,1},{16,22},{17,23},{1... | collective-permute-start | bytes 1179656 | tf_op jit(solution)/shard_map/cond/branch_1_fun/ppermute | solution.py:361
  86.7 41.9 %collective-permute-start.43 = (bf16[8,2,32,384]{3,2,1,0:T(8,128)(2,1)}, bf16[8,2,32,384]{3,2,1,0:T(8,128)(2,1)S(1)}, u32[]{:S(2)}, u32[]{:S(2)}) collective-permute-start(bf16[8,2,32,384]{3,2,1,0:T(8,128)(2,1)} %get-tuple-element.196), channel_id=1, source_target_pairs={{0,1},{1,0},{2,3},{3,2},{4,5},{5,4},{6,7},{7,6},{16,17},{17,16},{1... | collective-permute-start | bytes 1179656 | tf_op jit(solution)/shard_map/cond/branch_1_fun/ppermute | solution.py:361
  88.6 39.9 %collective-permute-start.44 = (bf16[8,2,32,384]{3,2,1,0:T(8,128)(2,1)}, bf16[8,2,32,384]{3,2,1,0:T(8,128)(2,1)S(1)}, u32[]{:S(2)}, u32[]{:S(2)}) collective-permute-start(bf16[8,2,32,384]{3,2,1,0:T(8,128)(2,1)} %get-tuple-element.197), channel_id=1, source_target_pairs={{0,11},{1,10},{2,9},{3,8},{8,3},{9,2},{10,1},{11,0},{16,27},{17,26... | collective-permute-start | bytes 1179656 | tf_op jit(solution)/shard_map/cond/branch_1_fun/ppermute | solution.py:361
  89.3 39.2 %collective-permute-start.45 = (bf16[8,2,32,384]{3,2,1,0:T(8,128)(2,1)}, bf16[8,2,32,384]{3,2,1,0:T(8,128)(2,1)S(1)}, u32[]{:S(2)}, u32[]{:S(2)}) collective-permute-start(bf16[8,2,32,384]{3,2,1,0:T(8,128)(2,1)} %get-tuple-element.198), channel_id=1, source_target_pairs={{0,7},{1,6},{2,5},{3,4},{4,3},{5,2},{6,1},{7,0},{16,23},{17,22},{1... | collective-permute-start | bytes 1179656 | tf_op jit(solution)/shard_map/cond/branch_1_fun/ppermute | solution.py:361
  95.2 43.0 %collective-permute-start.46 = (bf16[8,2,32,384]{3,2,1,0:T(8,128)(2,1)}, bf16[8,2,32,384]{3,2,1,0:T(8,128)(2,1)S(1)}, u32[]{:S(2)}, u32[]{:S(2)}) collective-permute-start(bf16[8,2,32,384]{3,2,1,0:T(8,128)(2,1)} %get-tuple-element.199), channel_id=1, source_target_pairs={{0,15},{1,14},{3,12},{4,11},{5,10},{7,8},{8,7},{9,6},{11,4},{12,3}... | collective-permute-start | bytes 1179656 | tf_op jit(solution)/shard_map/cond/branch_1_fun/ppermute | solution.py:361
  158.8 43.0 %collective-permute-start.48 = (bf16[8,2,32,384]{3,2,1,0:T(8,128)(2,1)}, bf16[8,2,32,384]{3,2,1,0:T(8,128)(2,1)S(1)}, u32[]{:S(2)}, u32[]{:S(2)}) collective-permute-start(bf16[8,2,32,384]{3,2,1,0:T(8,128)(2,1)} %get-tuple-element.204), channel_id=1, source_target_pairs={{0,4},{1,5},{2,6},{3,7},{4,0},{5,1},{6,2},{7,3},{16,20},{17,21},{1... | collective-permute-start | bytes 1179656 | tf_op jit(solution)/shard_map/cond/branch_1_fun/ppermute | solution.py:361
  181.9 48.5 %collective-permute-start.52 = (bf16[8,2,32,384]{3,2,1,0:T(8,128)(2,1)}, bf16[8,2,32,384]{3,2,1,0:T(8,128)(2,1)S(1)}, u32[]{:S(2)}, u32[]{:S(2)}) collective-permute-start(bf16[8,2,32,384]{3,2,1,0:T(8,128)(2,1)} %get-tuple-element.208), channel_id=1, source_target_pairs={{0,5},{1,4},{2,7},{3,6},{4,1},{5,0},{6,3},{7,2},{16,21},{17,20},{1... | collective-permute-start | bytes 1179656 | tf_op jit(solution)/shard_map/cond/branch_1_fun/ppermute | solution.py:361
  201.8 29.9 %collective-permute-start.53 = (bf16[8,2,32,384]{3,2,1,0:T(8,128)(2,1)}, bf16[8,2,32,384]{3,2,1,0:T(8,128)(2,1)S(1)}, u32[]{:S(2)}, u32[]{:S(2)}) collective-permute-start(bf16[8,2,32,384]{3,2,1,0:T(8,128)(2,1)} %get-tuple-element.209), channel_id=1, source_target_pairs={{0,13},{1,12},{2,15},{3,14},{4,9},{5,8},{6,11},{7,10},{8,5},{9,4},... | collective-permute-start | bytes 1179656 | tf_op jit(solution)/shard_map/cond/branch_1_fun/ppermute | solution.py:361
  201.8 35.2 %collective-permute-start.54 = (bf16[8,2,32,384]{3,2,1,0:T(8,128)(2,1)}, bf16[8,2,32,384]{3,2,1,0:T(8,128)(2,1)}, u32[]{:S(2)}, u32[]{:S(2)}) collective-permute-start(bf16[8,2,32,384]{3,2,1,0:T(8,128)(2,1)} %get-tuple-element.210), channel_id=1, source_target_pairs={{0,2},{1,3},{2,0},{3,1},{4,6},{5,7},{6,4},{7,5},{16,18},{17,19},{1... | collective-permute-start | bytes 1179656 | tf_op jit(solution)/shard_map/cond/branch_1_fun/ppermute | solution.py:361
  203.7 34.7 %collective-permute-start.55 = (bf16[8,2,32,384]{3,2,1,0:T(8,128)(2,1)}, bf16[8,2,32,384]{3,2,1,0:T(8,128)(2,1)}, u32[]{:S(2)}, u32[]{:S(2)}) collective-permute-start(bf16[8,2,32,384]{3,2,1,0:T(8,128)(2,1)} %get-tuple-element.211), channel_id=1, source_target_pairs={{0,10},{1,11},{2,8},{3,9},{8,2},{9,3},{10,0},{11,1},{16,26},{17,27... | collective-permute-start | bytes 1179656 | tf_op jit(solution)/shard_map/cond/branch_1_fun/ppermute | solution.py:361
  205.2 52.8 %collective-permute-start.56 = (bf16[8,2,32,384]{3,2,1,0:T(8,128)(2,1)}, bf16[8,2,32,384]{3,2,1,0:T(8,128)(2,1)}, u32[]{:S(2)}, u32[]{:S(2)}) collective-permute-start(bf16[8,2,32,384]{3,2,1,0:T(8,128)(2,1)} %get-tuple-element.212), channel_id=1, source_target_pairs={{0,6},{1,7},{2,4},{3,5},{4,2},{5,3},{6,0},{7,1},{16,22},{17,23},{1... | collective-permute-start | bytes 1179656 | tf_op jit(solution)/shard_map/cond/branch_1_fun/ppermute | solution.py:361
  213.1 46.9 %all-to-all-start.1 = ((f32[16,24,128]{2,1,0:T(8,128)}), f32[16,24,128]{2,1,0:T(8,128)S(1)}, u32[]{:S(2)}, u32[]{:S(2)}) async-start(f32[16,24,128]{2,1,0:T(8,128)} %broadcast_in_dim.11), calls=%async_computation.1 | async-start | bytes 393216 | tf_op jit(solution)/shard_map/cond/branch_1_fun/all_to_all | solution.py:415
  230.4 34.7 %collective-permute-start.57 = (bf16[8,2,32,384]{3,2,1,0:T(8,128)(2,1)}, bf16[8,2,32,384]{3,2,1,0:T(8,128)(2,1)}, u32[]{:S(2)}, u32[]{:S(2)}) collective-permute-start(bf16[8,2,32,384]{3,2,1,0:T(8,128)(2,1)} %get-tuple-element.213), channel_id=1, source_target_pairs={{0,14},{2,12},{3,13},{4,10},{6,8},{7,9},{8,6},{10,4},{11,5},{12,2}... | collective-permute-start | bytes 1179656 | tf_op jit(solution)/shard_map/cond/branch_1_fun/ppermute | solution.py:361
  231.7 33.3 %collective-permute-start.58 = (bf16[8,2,32,384]{3,2,1,0:T(8,128)(2,1)}, bf16[8,2,32,384]{3,2,1,0:T(8,128)(2,1)}, u32[]{:S(2)}, u32[]{:S(2)}) collective-permute-start(bf16[8,2,32,384]{3,2,1,0:T(8,128)(2,1)} %get-tuple-element.214), channel_id=1, source_target_pairs={{0,1},{1,0},{2,3},{3,2},{4,5},{5,4},{6,7},{7,6},{16,17},{17,16},{1... | collective-permute-start | bytes 1179656 | tf_op jit(solution)/shard_map/cond/branch_1_fun/ppermute | solution.py:361
  237.0 28.0 %collective-permute-start.59 = (bf16[8,2,32,384]{3,2,1,0:T(8,128)(2,1)}, bf16[8,2,32,384]{3,2,1,0:T(8,128)(2,1)}, u32[]{:S(2)}, u32[]{:S(2)}) collective-permute-start(bf16[8,2,32,384]{3,2,1,0:T(8,128)(2,1)} %get-tuple-element.215), channel_id=1, source_target_pairs={{0,11},{1,10},{2,9},{3,8},{8,3},{9,2},{10,1},{11,0},{16,27},{17,26... | collective-permute-start | bytes 1179656 | tf_op jit(solution)/shard_map/cond/branch_1_fun/ppermute | solution.py:361
  238.4 33.2 %collective-permute-start.60 = (bf16[8,2,32,384]{3,2,1,0:T(8,128)(2,1)}, bf16[8,2,32,384]{3,2,1,0:T(8,128)(2,1)}, u32[]{:S(2)}, u32[]{:S(2)}) collective-permute-start(bf16[8,2,32,384]{3,2,1,0:T(8,128)(2,1)} %get-tuple-element.216), channel_id=1, source_target_pairs={{0,7},{1,6},{2,5},{3,4},{4,3},{5,2},{6,1},{7,0},{16,23},{17,22},{1... | collective-permute-start | bytes 1179656 | tf_op jit(solution)/shard_map/cond/branch_1_fun/ppermute | solution.py:361
  (36 other events, 1685.9 us)

commit v3 on v2

--- a/solution.py
+++ b/solution.py
@@ -163,7 +163,7 @@
 
     mean = lax.fori_loop(0, STEPS, one, jnp.zeros((1, width), F32), unroll=unroll)
     mean = mean * (0.5 / half)
-    mean_ref[0] = jnp.broadcast_to(mean, mean_ref.shape[1:])
+    mean_ref[0] = mean
     centre = minus[0:1, :] - mean
 
     def two(t, carry):
@@ -217,7 +217,7 @@
                 pl.BlockSpec((2, lanes), whole),
             ]
             + [block] * devices,
-            out_specs=[block] * devices + [pl.BlockSpec((1, 8, width), lambda q, s: (q, 0, 0))],
+            out_specs=[block] * devices + [pl.BlockSpec((1, 1, width), lambda q, s: (q, 0, 0))],
             scratch_shapes=[
                 pltpu.VMEM((2 * total, width), BF16),
                 pltpu.VMEM((half, width), F32),
@@ -227,7 +227,7 @@
             ],
         ),
         out_shape=[jax.ShapeDtypeStruct(blocks[0].shape, BF16)] * devices
-        + [jax.ShapeDtypeStruct((pairs // count, 8, width), F32)],
+        + [jax.ShapeDtypeStruct((pairs // count, 1, width), F32)],
         compiler_params=params(),
         name="grid",
     )(pos, cosine, sine, middle, mix, coef, *blocks)
@@ -410,7 +410,7 @@
         )
         parts = exchange(parts, devices, home)
 
-        sent = means[:, 0].reshape(1, -1, LANES)
+        sent = means.reshape(1, -1, LANES)
         sent = jnp.broadcast_to(sent, (devices,) + sent.shape[1:])
         every = lax.all_to_all(sent, "wave", split_axis=0, concat_axis=0, tiled=True)
         every = every.reshape(devices * pairs, 4 * levels)

time: 298 us -> 298 us (level)
  no operation moved by 1% of the time
where the time goes in v3:
time: 298 us; the launch traced here: 296 us
  starting transfers between devices  173 us (58%)
  waiting for transfers between devices  52.2 us (18%)
  Pallas kernels  45.7 us (15%)
  local copies, waits for them, and re-layouts  12.3 us (4%)
  other arithmetic  11.2 us (4%)
    ppermute x30, starting transfers between devices, exchange(): array = lax.ppermute(array, 'wave', pairs)  148 us
    ppermute x30, waiting for transfers between devices, exchange(): array = lax.ppermute(array, 'wave', pairs)  52.2 us
    pallas_call x1, Pallas kernels, on_grid(): pl.pallas_call(functools.partial(grid_kernel, devices, waves, unroll), gr...  19.2 us
    all_to_all x1, starting transfers between devices, finish(): lax.all_to_all(sent, 'wave', split_axis=0, concat_axis=0, tiled=True)  16.1 us
    pallas_call x1, Pallas kernels, inverse(): pl.pallas_call(functools.partial(inverse_kernel, devices, group, waves, u...  14.8 us
    pallas_call x1, Pallas kernels, forward(): pl.pallas_call(functools.partial(forward_kernel, devices, group, waves),...  11.7 us
    ppermute x1, starting transfers between devices, exchange(): lax.ppermute(arrays[order.index(far)], 'wave', [(d, d ^ hop) for d in han...  7.08 us
  transfers between devices with their start and end apart: 33, of which 8 were waited for; matrix products, arithmetic and copies ran while one was open for 7% of the time, Pallas kernels for 0%

profile of v3, /device:TPU:9, one launch (start us, length us, event | category | flops | bytes accessed | tf_op | source)
XLA Modules:
  0.0 296.4 jit_solution(8278861743133425973)
XLA Ops:
  2.1 11.7 %forward.1 = (bf16[8,2,32,384]{3,2,1,0:T(8,128)(2,1)S(1)}, bf16[8,2,32,384]{3,2,1,0:T(8,128)(2,1)}, bf16[8,2,32,384]{3,2,1,0:T(8,128)(2,1)}, bf16[8,2,32,384]{3,...) custom-call(s32[1]{0:T(128)} %bitcast.12.pos_ref, ...), custom_call_target="tpu_custom_call" | custom-call | tf_op jit(solution)/shard_map/forward/pallas_call | solution.py:102
  13.8 282.4 %conditional.1 = (bf16[32,2,192,256]{3,2,1,0:T(8,128)(2,1)}) conditional(s32[]{:T(128)} %convert_element_type.121, (s32[]{:T(128)}, f32[96,96]{1,0:T(8,128)S(1)}, f32[96]{0:T(128)}, f32[96]{0:T(128)}, bf16[8,2,32,384]{3,2,1,0:T(8,128)(2,1)}, /*index=5*/bf16[8,2,32,384]{3,2,1,0:T(8,128)(2,1)}, bf16[8,2,32,384]{3,2,1,0:T(8,128)(2,1)}, ...), branch_computations={%region_1.5_spmd, %region_5.9_spmd} | conditional | flops 3923156 | bytes 84530384 | solution.py:430
  14.5 5.6 %collective-permute-start.31 = (bf16[8,2,32,384]{3,2,1,0:T(8,128)(2,1)}, bf16[8,2,32,384]{3,2,1,0:T(8,128)(2,1)S(1)}, u32[]{:S(2)}, u32[]{:S(2)}) collective-permute-start(bf16[8,2,32,384]{3,2,1,0:T(8,128)(2,1)} %get-tuple-element.186), channel_id=1, source_target_pairs={{0,4},{1,5},{2,6},{3,7},{4,0},{5,1},{6,2},{7,3},{16,20},{17,21},{1... | collective-permute-start | bytes 1179656 | tf_op jit(solution)/shard_map/cond/branch_1_fun/ppermute | solution.py:361
  22.1 4.3 %collective-permute-start.33 = (bf16[8,2,32,384]{3,2,1,0:T(8,128)(2,1)}, bf16[8,2,32,384]{3,2,1,0:T(8,128)(2,1)S(1)}, u32[]{:S(2)}, u32[]{:S(2)}) collective-permute-start(bf16[8,2,32,384]{3,2,1,0:T(8,128)(2,1)} %get-tuple-element.188), channel_id=1, source_target_pairs={{0,3},{1,2},{2,1},{3,0},{4,7},{5,6},{6,5},{7,4},{16,19},{17,18},{1... | collective-permute-start | bytes 1179656 | tf_op jit(solution)/shard_map/cond/branch_1_fun/ppermute | solution.py:361
  30.1 13.8 %collective-permute-start.35 = (bf16[8,2,32,384]{3,2,1,0:T(8,128)(2,1)}, bf16[8,2,32,384]{3,2,1,0:T(8,128)(2,1)S(1)}, u32[]{:S(2)}, u32[]{:S(2)}) collective-permute-start(bf16[8,2,32,384]{3,2,1,0:T(8,128)(2,1)} %get-tuple-element.190), channel_id=1, source_target_pairs={{0,5},{1,4},{2,7},{3,6},{4,1},{5,0},{6,3},{7,2},{16,21},{17,20},{1... | collective-permute-start | bytes 1179656 | tf_op jit(solution)/shard_map/cond/branch_1_fun/ppermute | solution.py:361
  43.9 7.1 %collective-permute-start.41 = (bf16[8,2,32,384]{3,2,1,0:T(8,128)(2,1)}, bf16[8,2,32,384]{3,2,1,0:T(8,128)(2,1)}, u32[]{:S(2)}, u32[]{:S(2)}) collective-permute-start(bf16[8,2,32,384]{3,2,1,0:T(8,128)(2,1)} %get-tuple-element.195), channel_id=1, source_target_pairs={{0,2},{1,3},{4,6},{5,7},{8,10},{9,11},{12,14},{13,15},{16,18},{17,... | collective-permute-start | bytes 1179656 | tf_op jit(solution)/shard_map/cond/branch_1_fun/ppermute | solution.py:355
  54.2 6.2 %collective-permute-start.36 = (bf16[8,2,32,384]{3,2,1,0:T(8,128)(2,1)}, bf16[8,2,32,384]{3,2,1,0:T(8,128)(2,1)}, u32[]{:S(2)}, u32[]{:S(2)}) collective-permute-start(bf16[8,2,32,384]{3,2,1,0:T(8,128)(2,1)} %get-tuple-element.191), channel_id=1, source_target_pairs={{0,13},{1,12},{2,15},{3,14},{4,9},{5,8},{6,11},{7,10},{8,5},{9,4},... | collective-permute-start | bytes 1179656 | tf_op jit(solution)/shard_map/cond/branch_1_fun/ppermute | solution.py:361
  60.4 4.2 %collective-permute-start.37 = (bf16[8,2,32,384]{3,2,1,0:T(8,128)(2,1)}, bf16[8,2,32,384]{3,2,1,0:T(8,128)(2,1)}, u32[]{:S(2)}, u32[]{:S(2)}) collective-permute-start(bf16[8,2,32,384]{3,2,1,0:T(8,128)(2,1)} %get-tuple-element.192), channel_id=1, source_target_pairs={{0,2},{1,3},{2,0},{3,1},{4,6},{5,7},{6,4},{7,5},{16,18},{17,19},{1... | collective-permute-start | bytes 1179656 | tf_op jit(solution)/shard_map/cond/branch_1_fun/ppermute | solution.py:361
  64.6 4.6 %collective-permute-done.35.rest_6_ = bf16[8,2,32,384]{3,2,1,0:T(8,128)(2,1)S(1)} collective-permute-done((bf16[8,2,32,384]{3,2,1,0:T(8,128)(2,1)}, bf16[8,2,32,384]{3,2,1,0:T(8,128)(2,1)S(1)}, u32[]{:S(2)}, u32[]{:S(2)}) %collective-permute-start.35) | collective-permute-done | bytes 393248 | tf_op jit(solution)/shard_map/cond/branch_1_fun/ppermute | solution.py:361
  80.0 4.8 %collective-permute-done.36.rest_7_ = bf16[8,2,32,384]{3,2,1,0:T(8,128)(2,1)} collective-permute-done((bf16[8,2,32,384]{3,2,1,0:T(8,128)(2,1)}, bf16[8,2,32,384]{3,2,1,0:T(8,128)(2,1)}, u32[]{:S(2)}, u32[]{:S(2)}) %collective-permute-start.36) | collective-permute-done | bytes 393248 | tf_op jit(solution)/shard_map/cond/branch_1_fun/ppermute | solution.py:361
  89.3 5.9 %collective-permute-start.45 = (bf16[8,2,32,384]{3,2,1,0:T(8,128)(2,1)}, bf16[8,2,32,384]{3,2,1,0:T(8,128)(2,1)S(1)}, u32[]{:S(2)}, u32[]{:S(2)}) collective-permute-start(bf16[8,2,32,384]{3,2,1,0:T(8,128)(2,1)} %get-tuple-element.198), channel_id=1, source_target_pairs={{0,7},{1,6},{2,5},{3,4},{4,3},{5,2},{6,1},{7,0},{16,23},{17,22},{1... | collective-permute-start | bytes 1179656 | tf_op jit(solution)/shard_map/cond/branch_1_fun/ppermute | solution.py:361
  95.2 30.1 %collective-permute-start.46 = (bf16[8,2,32,384]{3,2,1,0:T(8,128)(2,1)}, bf16[8,2,32,384]{3,2,1,0:T(8,128)(2,1)S(1)}, u32[]{:S(2)}, u32[]{:S(2)}) collective-permute-start(bf16[8,2,32,384]{3,2,1,0:T(8,128)(2,1)} %get-tuple-element.199), channel_id=1, source_target_pairs={{0,15},{1,14},{3,12},{4,11},{5,10},{7,8},{8,7},{9,6},{11,4},{12,3}... | collective-permute-start | bytes 1179656 | tf_op jit(solution)/shard_map/cond/branch_1_fun/ppermute | solution.py:361
  128.6 9.6 %collective-permute-done.46.rest_15_ = bf16[8,2,32,384]{3,2,1,0:T(8,128)(2,1)S(1)} collective-permute-done((bf16[8,2,32,384]{3,2,1,0:T(8,128)(2,1)}, bf16[8,2,32,384]{3,2,1,0:T(8,128)(2,1)S(1)}, u32[]{:S(2)}, u32[]{:S(2)}) %collective-permute-start.46) | collective-permute-done | bytes 393248 | tf_op jit(solution)/shard_map/cond/branch_1_fun/ppermute | solution.py:361
  139.0 19.2 %grid.3 = (bf16[8,2,32,384]{3,2,1,0:T(8,128)(2,1)}, bf16[8,2,32,384]{3,2,1,0:T(8,128)(2,1)}, bf16[8,2,32,384]{3,2,1,0:T(8,128)(2,1)}, bf16[8,2,32,384]{3,2,1,0:T...) custom-call(s32[1]{0:T(128)} %get-tuple-element.169.pos_ref, ...), custom_call_target="tpu_custom_call" | custom-call | tf_op jit(solution)/shard_map/cond/branch_1_fun/grid/pallas_call | solution.py:207
  158.9 17.3 %collective-permute-start.48 = (bf16[8,2,32,384]{3,2,1,0:T(8,128)(2,1)}, bf16[8,2,32,384]{3,2,1,0:T(8,128)(2,1)S(1)}, u32[]{:S(2)}, u32[]{:S(2)}) collective-permute-start(bf16[8,2,32,384]{3,2,1,0:T(8,128)(2,1)} %get-tuple-element.204), channel_id=1, source_target_pairs={{0,4},{1,5},{2,6},{3,7},{4,0},{5,1},{6,2},{7,3},{16,20},{17,21},{1... | collective-permute-start | bytes 1179656 | tf_op jit(solution)/shard_map/cond/branch_1_fun/ppermute | solution.py:361
  181.9 16.5 %collective-permute-start.52 = (bf16[8,2,32,384]{3,2,1,0:T(8,128)(2,1)}, bf16[8,2,32,384]{3,2,1,0:T(8,128)(2,1)S(1)}, u32[]{:S(2)}, u32[]{:S(2)}) collective-permute-start(bf16[8,2,32,384]{3,2,1,0:T(8,128)(2,1)} %get-tuple-element.208), channel_id=1, source_target_pairs={{0,5},{1,4},{2,7},{3,6},{4,1},{5,0},{6,3},{7,2},{16,21},{17,20},{1... | collective-permute-start | bytes 1179656 | tf_op jit(solution)/shard_map/cond/branch_1_fun/ppermute | solution.py:361
  205.2 6.2 %collective-permute-start.56 = (bf16[8,2,32,384]{3,2,1,0:T(8,128)(2,1)}, bf16[8,2,32,384]{3,2,1,0:T(8,128)(2,1)}, u32[]{:S(2)}, u32[]{:S(2)}) collective-permute-start(bf16[8,2,32,384]{3,2,1,0:T(8,128)(2,1)} %get-tuple-element.212), channel_id=1, source_target_pairs={{0,6},{1,7},{2,4},{3,5},{4,2},{5,3},{6,0},{7,1},{16,22},{17,23},{1... | collective-permute-start | bytes 1179656 | tf_op jit(solution)/shard_map/cond/branch_1_fun/ppermute | solution.py:361
  213.0 16.1 %all-to-all-start.1 = ((f32[16,24,128]{2,1,0:T(8,128)}), f32[16,24,128]{2,1,0:T(8,128)S(1)}, u32[]{:S(2)}, u32[]{:S(2)}) async-start(f32[16,24,128]{2,1,0:T(8,128)} %broadcast_in_dim.11), calls=%async_computation.1 | async-start | bytes 393216 | tf_op jit(solution)/shard_map/cond/branch_1_fun/all_to_all | solution.py:415
  231.5 5.3 %collective-permute-start.58 = (bf16[8,2,32,384]{3,2,1,0:T(8,128)(2,1)}, bf16[8,2,32,384]{3,2,1,0:T(8,128)(2,1)}, u32[]{:S(2)}, u32[]{:S(2)}) collective-permute-start(bf16[8,2,32,384]{3,2,1,0:T(8,128)(2,1)} %get-tuple-element.214), channel_id=1, source_target_pairs={{0,1},{1,0},{2,3},{3,2},{4,5},{5,4},{6,7},{7,6},{16,17},{17,16},{1... | collective-permute-start | bytes 1179656 | tf_op jit(solution)/shard_map/cond/branch_1_fun/ppermute | solution.py:361
  238.3 9.5 %collective-permute-start.60 = (bf16[8,2,32,384]{3,2,1,0:T(8,128)(2,1)}, bf16[8,2,32,384]{3,2,1,0:T(8,128)(2,1)}, u32[]{:S(2)}, u32[]{:S(2)}) collective-permute-start(bf16[8,2,32,384]{3,2,1,0:T(8,128)(2,1)} %get-tuple-element.216), channel_id=1, source_target_pairs={{0,7},{1,6},{2,5},{3,4},{4,3},{5,2},{6,1},{7,0},{16,23},{17,22},{1... | collective-permute-start | bytes 1179656 | tf_op jit(solution)/shard_map/cond/branch_1_fun/ppermute | solution.py:361
  247.7 10.3 %collective-permute-done.56.rest_10_ = bf16[8,2,32,384]{3,2,1,0:T(8,128)(2,1)} collective-permute-done((bf16[8,2,32,384]{3,2,1,0:T(8,128)(2,1)}, bf16[8,2,32,384]{3,2,1,0:T(8,128)(2,1)}, u32[]{:S(2)}, u32[]{:S(2)}) %collective-permute-start.56) | collective-permute-done | bytes 393248 | tf_op jit(solution)/shard_map/cond/branch_1_fun/ppermute | solution.py:361
  264.9 6.8 %collective-permute-done.60.rest_14_ = bf16[8,2,32,384]{3,2,1,0:T(8,128)(2,1)} collective-permute-done((bf16[8,2,32,384]{3,2,1,0:T(8,128)(2,1)}, bf16[8,2,32,384]{3,2,1,0:T(8,128)(2,1)}, u32[]{:S(2)}, u32[]{:S(2)}) %collective-permute-start.60) | collective-permute-done | bytes 393248 | tf_op jit(solution)/shard_map/cond/branch_1_fun/ppermute | solution.py:361
  271.7 9.5 %collective-permute-done.61.rest_15_ = bf16[8,2,32,384]{3,2,1,0:T(8,128)(2,1)} collective-permute-done((bf16[8,2,32,384]{3,2,1,0:T(8,128)(2,1)}, bf16[8,2,32,384]{3,2,1,0:T(8,128)(2,1)}, u32[]{:S(2)}, u32[]{:S(2)}) %collective-permute-start.61) | collective-permute-done | bytes 393248 | tf_op jit(solution)/shard_map/cond/branch_1_fun/ppermute | solution.py:361
  281.2 14.8 %inverse.3 = bf16[32,2,192,256]{3,2,1,0:T(8,128)(2,1)} custom-call(s32[1]{0:T(128)} %get-tuple-element.169.pos_ref, f32[64]{0:T(128)} %reshape.552.sums_ref, bf16[32,2,192,256]{3,2,1,0:T(8,128)(2,1)} %get-tuple-element.175.spec_ref, bf16[32,2,256,256]{3,2,1,0:T(8,128)(2,1)} %get-tuple-element.176.basis_ref, s32[1,256]{1,0:T(1,128)S(1)} %get-tuple-element.177.trunc_ref, ...), custom_call_target="tpu_custom_call" | custom-call | tf_op jit(solution)/shard_map/cond/branch_1_fun/inverse/pallas_call | solution.py:303
  (164 shorter events, 54.8 us)
Async XLA Ops:
  14.5 29.3 %collective-permute-start.31 = (bf16[8,2,32,384]{3,2,1,0:T(8,128)(2,1)}, bf16[8,2,32,384]{3,2,1,0:T(8,128)(2,1)S(1)}, u32[]{:S(2)}, u32[]{:S(2)}) collective-permute-start(bf16[8,2,32,384]{3,2,1,0:T(8,128)(2,1)} %get-tuple-element.186), channel_id=1, source_target_pairs={{0,4},{1,5},{2,6},{3,7},{4,0},{5,1},{6,2},{7,3},{16,20},{17,21},{1... | collective-permute-start | bytes 1179656 | tf_op jit(solution)/shard_map/cond/branch_1_fun/ppermute | solution.py:361
  20.2 32.6 %collective-permute-start.32 = (bf16[8,2,32,384]{3,2,1,0:T(8,128)(2,1)}, bf16[8,2,32,384]{3,2,1,0:T(8,128)(2,1)S(1)}, u32[]{:S(2)}, u32[]{:S(2)}) collective-permute-start(bf16[8,2,32,384]{3,2,1,0:T(8,128)(2,1)} %get-tuple-element.187), channel_id=1, source_target_pairs={{0,12},{1,13},{2,14},{4,8},{5,9},{6,10},{8,4},{9,5},{10,6},{12,0},... | collective-permute-start | bytes 1179656 | tf_op jit(solution)/shard_map/cond/branch_1_fun/ppermute | solution.py:361
  22.1 32.1 %collective-permute-start.33 = (bf16[8,2,32,384]{3,2,1,0:T(8,128)(2,1)}, bf16[8,2,32,384]{3,2,1,0:T(8,128)(2,1)S(1)}, u32[]{:S(2)}, u32[]{:S(2)}) collective-permute-start(bf16[8,2,32,384]{3,2,1,0:T(8,128)(2,1)} %get-tuple-element.188), channel_id=1, source_target_pairs={{0,3},{1,2},{2,1},{3,0},{4,7},{5,6},{6,5},{7,4},{16,19},{17,18},{1... | collective-permute-start | bytes 1179656 | tf_op jit(solution)/shard_map/cond/branch_1_fun/ppermute | solution.py:361
  26.4 34.1 %collective-permute-start.34 = (bf16[8,2,32,384]{3,2,1,0:T(8,128)(2,1)}, bf16[8,2,32,384]{3,2,1,0:T(8,128)(2,1)S(1)}, u32[]{:S(2)}, u32[]{:S(2)}) collective-permute-start(bf16[8,2,32,384]{3,2,1,0:T(8,128)(2,1)} %get-tuple-element.189), channel_id=1, source_target_pairs={{0,9},{1,8},{2,11},{3,10},{8,1},{9,0},{10,3},{11,2},{16,25},{17,24... | collective-permute-start | bytes 1179656 | tf_op jit(solution)/shard_map/cond/branch_1_fun/ppermute | solution.py:361
  30.1 39.2 %collective-permute-start.35 = (bf16[8,2,32,384]{3,2,1,0:T(8,128)(2,1)}, bf16[8,2,32,384]{3,2,1,0:T(8,128)(2,1)S(1)}, u32[]{:S(2)}, u32[]{:S(2)}) collective-permute-start(bf16[8,2,32,384]{3,2,1,0:T(8,128)(2,1)} %get-tuple-element.190), channel_id=1, source_target_pairs={{0,5},{1,4},{2,7},{3,6},{4,1},{5,0},{6,3},{7,2},{16,21},{17,20},{1... | collective-permute-start | bytes 1179656 | tf_op jit(solution)/shard_map/cond/branch_1_fun/ppermute | solution.py:361
  43.9 26.8 %collective-permute-start.41 = (bf16[8,2,32,384]{3,2,1,0:T(8,128)(2,1)}, bf16[8,2,32,384]{3,2,1,0:T(8,128)(2,1)}, u32[]{:S(2)}, u32[]{:S(2)}) collective-permute-start(bf16[8,2,32,384]{3,2,1,0:T(8,128)(2,1)} %get-tuple-element.195), channel_id=1, source_target_pairs={{0,2},{1,3},{4,6},{5,7},{8,10},{9,11},{12,14},{13,15},{16,18},{17,... | collective-permute-start | bytes 1179656 | tf_op jit(solution)/shard_map/cond/branch_1_fun/ppermute | solution.py:355
  52.8 36.5 %collective-permute-start.40 = (bf16[8,2,32,384]{3,2,1,0:T(8,128)(2,1)}, bf16[8,2,32,384]{3,2,1,0:T(8,128)(2,1)}, u32[]{:S(2)}, u32[]{:S(2)}) collective-permute-start(bf16[8,2,32,384]{3,2,1,0:T(8,128)(2,1)} %get-tuple-element.195), channel_id=1, source_target_pairs={{2,12},{6,8},{10,4},{14,0},{18,28},{22,24},{26,20},{30,16}} | collective-permute-start | bytes 1179656 | tf_op jit(solution)/shard_map/cond/branch_1_fun/ppermute | solution.py:361
  54.2 30.5 %collective-permute-start.36 = (bf16[8,2,32,384]{3,2,1,0:T(8,128)(2,1)}, bf16[8,2,32,384]{3,2,1,0:T(8,128)(2,1)}, u32[]{:S(2)}, u32[]{:S(2)}) collective-permute-start(bf16[8,2,32,384]{3,2,1,0:T(8,128)(2,1)} %get-tuple-element.191), channel_id=1, source_target_pairs={{0,13},{1,12},{2,15},{3,14},{4,9},{5,8},{6,11},{7,10},{8,5},{9,4},... | collective-permute-start | bytes 1179656 | tf_op jit(solution)/shard_map/cond/branch_1_fun/ppermute | solution.py:361
  84.7 43.8 %collective-permute-start.39 = (bf16[8,2,32,384]{3,2,1,0:T(8,128)(2,1)}, bf16[8,2,32,384]{3,2,1,0:T(8,128)(2,1)S(1)}, u32[]{:S(2)}, u32[]{:S(2)}) collective-permute-start(bf16[8,2,32,384]{3,2,1,0:T(8,128)(2,1)} %get-tuple-element.194), channel_id=1, source_target_pairs={{0,6},{1,7},{2,4},{3,5},{4,2},{5,3},{6,0},{7,1},{16,22},{17,23},{1... | collective-permute-start | bytes 1179656 | tf_op jit(solution)/shard_map/cond/branch_1_fun/ppermute | solution.py:361
  86.7 41.9 %collective-permute-start.43 = (bf16[8,2,32,384]{3,2,1,0:T(8,128)(2,1)}, bf16[8,2,32,384]{3,2,1,0:T(8,128)(2,1)S(1)}, u32[]{:S(2)}, u32[]{:S(2)}) collective-permute-start(bf16[8,2,32,384]{3,2,1,0:T(8,128)(2,1)} %get-tuple-element.196), channel_id=1, source_target_pairs={{0,1},{1,0},{2,3},{3,2},{4,5},{5,4},{6,7},{7,6},{16,17},{17,16},{1... | collective-permute-start | bytes 1179656 | tf_op jit(solution)/shard_map/cond/branch_1_fun/ppermute | solution.py:361
  88.6 40.0 %collective-permute-start.44 = (bf16[8,2,32,384]{3,2,1,0:T(8,128)(2,1)}, bf16[8,2,32,384]{3,2,1,0:T(8,128)(2,1)S(1)}, u32[]{:S(2)}, u32[]{:S(2)}) collective-permute-start(bf16[8,2,32,384]{3,2,1,0:T(8,128)(2,1)} %get-tuple-element.197), channel_id=1, source_target_pairs={{0,11},{1,10},{2,9},{3,8},{8,3},{9,2},{10,1},{11,0},{16,27},{17,26... | collective-permute-start | bytes 1179656 | tf_op jit(solution)/shard_map/cond/branch_1_fun/ppermute | solution.py:361
  89.3 39.3 %collective-permute-start.45 = (bf16[8,2,32,384]{3,2,1,0:T(8,128)(2,1)}, bf16[8,2,32,384]{3,2,1,0:T(8,128)(2,1)S(1)}, u32[]{:S(2)}, u32[]{:S(2)}) collective-permute-start(bf16[8,2,32,384]{3,2,1,0:T(8,128)(2,1)} %get-tuple-element.198), channel_id=1, source_target_pairs={{0,7},{1,6},{2,5},{3,4},{4,3},{5,2},{6,1},{7,0},{16,23},{17,22},{1... | collective-permute-start | bytes 1179656 | tf_op jit(solution)/shard_map/cond/branch_1_fun/ppermute | solution.py:361
  95.2 43.0 %collective-permute-start.46 = (bf16[8,2,32,384]{3,2,1,0:T(8,128)(2,1)}, bf16[8,2,32,384]{3,2,1,0:T(8,128)(2,1)S(1)}, u32[]{:S(2)}, u32[]{:S(2)}) collective-permute-start(bf16[8,2,32,384]{3,2,1,0:T(8,128)(2,1)} %get-tuple-element.199), channel_id=1, source_target_pairs={{0,15},{1,14},{3,12},{4,11},{5,10},{7,8},{8,7},{9,6},{11,4},{12,3}... | collective-permute-start | bytes 1179656 | tf_op jit(solution)/shard_map/cond/branch_1_fun/ppermute | solution.py:361
  158.9 43.0 %collective-permute-start.48 = (bf16[8,2,32,384]{3,2,1,0:T(8,128)(2,1)}, bf16[8,2,32,384]{3,2,1,0:T(8,128)(2,1)S(1)}, u32[]{:S(2)}, u32[]{:S(2)}) collective-permute-start(bf16[8,2,32,384]{3,2,1,0:T(8,128)(2,1)} %get-tuple-element.204), channel_id=1, source_target_pairs={{0,4},{1,5},{2,6},{3,7},{4,0},{5,1},{6,2},{7,3},{16,20},{17,21},{1... | collective-permute-start | bytes 1179656 | tf_op jit(solution)/shard_map/cond/branch_1_fun/ppermute | solution.py:361
  181.9 48.3 %collective-permute-start.52 = (bf16[8,2,32,384]{3,2,1,0:T(8,128)(2,1)}, bf16[8,2,32,384]{3,2,1,0:T(8,128)(2,1)S(1)}, u32[]{:S(2)}, u32[]{:S(2)}) collective-permute-start(bf16[8,2,32,384]{3,2,1,0:T(8,128)(2,1)} %get-tuple-element.208), channel_id=1, source_target_pairs={{0,5},{1,4},{2,7},{3,6},{4,1},{5,0},{6,3},{7,2},{16,21},{17,20},{1... | collective-permute-start | bytes 1179656 | tf_op jit(solution)/shard_map/cond/branch_1_fun/ppermute | solution.py:361
  201.8 29.7 %collective-permute-start.53 = (bf16[8,2,32,384]{3,2,1,0:T(8,128)(2,1)}, bf16[8,2,32,384]{3,2,1,0:T(8,128)(2,1)S(1)}, u32[]{:S(2)}, u32[]{:S(2)}) collective-permute-start(bf16[8,2,32,384]{3,2,1,0:T(8,128)(2,1)} %get-tuple-element.209), channel_id=1, source_target_pairs={{0,13},{1,12},{2,15},{3,14},{4,9},{5,8},{6,11},{7,10},{8,5},{9,4},... | collective-permute-start | bytes 1179656 | tf_op jit(solution)/shard_map/cond/branch_1_fun/ppermute | solution.py:361
  201.8 35.0 %collective-permute-start.54 = (bf16[8,2,32,384]{3,2,1,0:T(8,128)(2,1)}, bf16[8,2,32,384]{3,2,1,0:T(8,128)(2,1)}, u32[]{:S(2)}, u32[]{:S(2)}) collective-permute-start(bf16[8,2,32,384]{3,2,1,0:T(8,128)(2,1)} %get-tuple-element.210), channel_id=1, source_target_pairs={{0,2},{1,3},{2,0},{3,1},{4,6},{5,7},{6,4},{7,5},{16,18},{17,19},{1... | collective-permute-start | bytes 1179656 | tf_op jit(solution)/shard_map/cond/branch_1_fun/ppermute | solution.py:361
  203.8 34.5 %collective-permute-start.55 = (bf16[8,2,32,384]{3,2,1,0:T(8,128)(2,1)}, bf16[8,2,32,384]{3,2,1,0:T(8,128)(2,1)}, u32[]{:S(2)}, u32[]{:S(2)}) collective-permute-start(bf16[8,2,32,384]{3,2,1,0:T(8,128)(2,1)} %get-tuple-element.211), channel_id=1, source_target_pairs={{0,10},{1,11},{2,8},{3,9},{8,2},{9,3},{10,0},{11,1},{16,26},{17,27... | collective-permute-start | bytes 1179656 | tf_op jit(solution)/shard_map/cond/branch_1_fun/ppermute | solution.py:361
  205.2 52.8 %collective-permute-start.56 = (bf16[8,2,32,384]{3,2,1,0:T(8,128)(2,1)}, bf16[8,2,32,384]{3,2,1,0:T(8,128)(2,1)}, u32[]{:S(2)}, u32[]{:S(2)}) collective-permute-start(bf16[8,2,32,384]{3,2,1,0:T(8,128)(2,1)} %get-tuple-element.212), channel_id=1, source_target_pairs={{0,6},{1,7},{2,4},{3,5},{4,2},{5,3},{6,0},{7,1},{16,22},{17,23},{1... | collective-permute-start | bytes 1179656 | tf_op jit(solution)/shard_map/cond/branch_1_fun/ppermute | solution.py:361
  213.0 47.1 %all-to-all-start.1 = ((f32[16,24,128]{2,1,0:T(8,128)}), f32[16,24,128]{2,1,0:T(8,128)S(1)}, u32[]{:S(2)}, u32[]{:S(2)}) async-start(f32[16,24,128]{2,1,0:T(8,128)} %broadcast_in_dim.11), calls=%async_computation.1 | async-start | bytes 393216 | tf_op jit(solution)/shard_map/cond/branch_1_fun/all_to_all | solution.py:415
  230.2 34.7 %collective-permute-start.57 = (bf16[8,2,32,384]{3,2,1,0:T(8,128)(2,1)}, bf16[8,2,32,384]{3,2,1,0:T(8,128)(2,1)}, u32[]{:S(2)}, u32[]{:S(2)}) collective-permute-start(bf16[8,2,32,384]{3,2,1,0:T(8,128)(2,1)} %get-tuple-element.213), channel_id=1, source_target_pairs={{0,14},{2,12},{3,13},{4,10},{6,8},{7,9},{8,6},{10,4},{11,5},{12,2}... | collective-permute-start | bytes 1179656 | tf_op jit(solution)/shard_map/cond/branch_1_fun/ppermute | solution.py:361
  231.5 33.3 %collective-permute-start.58 = (bf16[8,2,32,384]{3,2,1,0:T(8,128)(2,1)}, bf16[8,2,32,384]{3,2,1,0:T(8,128)(2,1)}, u32[]{:S(2)}, u32[]{:S(2)}) collective-permute-start(bf16[8,2,32,384]{3,2,1,0:T(8,128)(2,1)} %get-tuple-element.214), channel_id=1, source_target_pairs={{0,1},{1,0},{2,3},{3,2},{4,5},{5,4},{6,7},{7,6},{16,17},{17,16},{1... | collective-permute-start | bytes 1179656 | tf_op jit(solution)/shard_map/cond/branch_1_fun/ppermute | solution.py:361
  236.8 28.0 %collective-permute-start.59 = (bf16[8,2,32,384]{3,2,1,0:T(8,128)(2,1)}, bf16[8,2,32,384]{3,2,1,0:T(8,128)(2,1)}, u32[]{:S(2)}, u32[]{:S(2)}) collective-permute-start(bf16[8,2,32,384]{3,2,1,0:T(8,128)(2,1)} %get-tuple-element.215), channel_id=1, source_target_pairs={{0,11},{1,10},{2,9},{3,8},{8,3},{9,2},{10,1},{11,0},{16,27},{17,26... | collective-permute-start | bytes 1179656 | tf_op jit(solution)/shard_map/cond/branch_1_fun/ppermute | solution.py:361
  238.3 33.4 %collective-permute-start.60 = (bf16[8,2,32,384]{3,2,1,0:T(8,128)(2,1)}, bf16[8,2,32,384]{3,2,1,0:T(8,128)(2,1)}, u32[]{:S(2)}, u32[]{:S(2)}) collective-permute-start(bf16[8,2,32,384]{3,2,1,0:T(8,128)(2,1)} %get-tuple-element.216), channel_id=1, source_target_pairs={{0,7},{1,6},{2,5},{3,4},{4,3},{5,2},{6,1},{7,0},{16,23},{17,22},{1... | collective-permute-start | bytes 1179656 | tf_op jit(solution)/shard_map/cond/branch_1_fun/ppermute | solution.py:361
  (36 other events, 1684.7 us)
